TPU v7x, 32 devices: a whole 2x2x4 slice. The times are simulated.
32 devices in a mesh: ens: 2 (over y), lon: 4 (over z), lat: 2 (over x), ch: 2 (over core).
Axes of the slice: x: 2, y: 2, z: 4, core: 2. Of those that a mesh axis runs over, the one named last changes fastest.
Arguments:
- input_field: bfloat16 [256, 128, 128], P(('ens', 'lat', 'ch'), 'lon'), parts along dimension 0, may hold values from -6 to 6
- encoder_filter: bfloat16 [128, 4, 5], P(('lat', 'ch')), may hold values from -2.6875 to 2.6875
- row_owner: int32 [256], P(('ens', 'lat', 'ch')), parts along dimension 0, may hold values from 0 to 63, as said below
- encoder_weight: bfloat16 [512, 256], replicated, may hold values from -0.25 to 0.25
- disco_basis: bfloat16 [64, 4, 3, 17], P(('lat', 'ch')), may hold values from -1.5 to 1.5
- row_widths: int32 [64], P(('lat', 'ch')), may hold values from 1 to 8, as said below
- block_weights: bfloat16 [2, 1024, 256], replicated, may hold values from -0.1875 to 0.1875
- cotangent: bfloat16 [128, 64, 256], P(('ens', 'lat', 'ch'), 'lon'), parts along dimension 0, may hold values from -6 to 6
Outputs:
- state_out: bfloat16 [128, 64, 256], P(('ens', 'lat', 'ch'), 'lon'), parts along dimension 0
- latent_grad: bfloat16 [128, 64, 256], P(('ens', 'lat', 'ch'), 'lon'), parts along dimension 0
- block_grads: float32 [4, 1024, 256], P('ens', None, 'ch'), parts along dimension 0
- encoder_grad: float32 [1024, 256], P('ens', 'ch'), parts along dimension 0
There are 2 independent parts, one for each index of `ens`. A program takes and returns all parts, laid end to end along the dimension named above; an argument that names none is the same for every part. Nothing has to cross between parts.
Inputs may be any that keep to these rules, and one draw needn't show every extreme that they name: `row_owner`: input row p feeds latent row (p - 1) // 2, p // 2 or (p + 1) // 2, and every latent row is fed by 1 to 3 input rows. `row_widths`: the first and last rows have 8.
All inputs are finite; a program needn't handle non-finite values.
Results may differ from a plain program's by a relative error of at most 0.014.
Values may be sent and summed in bfloat16 or wider, within the bound.
A program may use at most 64 MiB of HBM per device.

v0:
```python
import math

import jax
import jax.numpy as jnp
from jax import lax
from jax.sharding import PartitionSpec as P

REACH = 8
TAP_REACH = 2


def passed_along(value, axis, steps):
    count = lax.axis_size(axis)
    pairs = [(source, (source + steps) % count) for source in range(count)]
    return lax.ppermute(value, axis, pairs)


def from_behind(block, axis, distance):
    devices = range(lax.axis_size(axis))
    route = [(i - distance, i) for i in devices if i - distance in devices]
    return lax.ppermute(block, axis, route)


def padded(block, sides, width, periodic):
    for axis, dim in sides:
        count = lax.axis_size(axis)
        forward = [(i, i + 1) for i in range(count - 1)]
        if periodic:
            forward.append((count - 1, 0))
        backward = [(target, source) for source, target in forward]
        low = lax.ppermute(
            lax.slice_in_dim(block, block.shape[dim] - width, None, axis=dim), axis, forward
        )
        high = lax.ppermute(lax.slice_in_dim(block, 0, width, axis=dim), axis, backward)
        block = jnp.concatenate([low, block, high], axis=dim)
    return block


def add_edges(middle, to_first, to_last):
    row_count = middle.shape[0]
    rest_pads = [(0, 0)] * (middle.ndim - 1)
    lower = jnp.pad(to_first, [(0, row_count - 1)] + rest_pads)
    upper = jnp.pad(to_last, [(row_count - 1, 0)] + rest_pads)
    return middle + lower + upper


def apply_basis(banded, extended, rows_dev):
    accumulated = None
    for shift_row in range(3):
        term = jnp.einsum(
            "ikjq,iqc->ijkc",
            banded[:, :, shift_row],
            extended[shift_row : shift_row + rows_dev],
            preferred_element_type=jnp.float32,
        )
        accumulated = term if accumulated is None else accumulated + term
    return accumulated


def spread_basis(banded, errors):
    pieces = [
        jnp.einsum(
            "ikjq,ijkc->iqc", banded[:, :, shift_row], errors, preferred_element_type=jnp.float32
        )
        for shift_row in range(3)
    ]
    first = jnp.pad(pieces[0], ((0, 2), (0, 0), (0, 0)))
    second = jnp.pad(pieces[1], ((1, 1), (0, 0), (0, 0)))
    third = jnp.pad(pieces[2], ((2, 0), (0, 0), (0, 0)))
    return first + second + third


def return_rims(spread, cols_dev):
    left_rim = spread[:, :REACH]
    right_rim = spread[:, REACH + cols_dev :]
    interior = spread[:, REACH : REACH + cols_dev]
    from_east = passed_along(left_rim.astype(jnp.bfloat16), "lon", -1).astype(left_rim.dtype)
    from_west = passed_along(right_rim.astype(jnp.bfloat16), "lon", 1).astype(right_rim.dtype)
    interior = interior + jnp.pad(from_west, ((0, 0), (0, cols_dev - REACH), (0, 0)))
    interior = interior + jnp.pad(from_east, ((0, 0), (cols_dev - REACH, 0), (0, 0)))
    row_total = interior.shape[0]
    from_above = from_behind(interior[0:1], ("lat", "ch"), -1)
    from_below = from_behind(interior[row_total - 1 :], ("lat", "ch"), 1)
    return add_edges(interior[1 : row_total - 1], from_below, from_above)


def per_device(
    input_field,
    encoder_filter,
    row_owner,
    encoder_weight,
    disco_basis,
    row_widths,
    block_weights,
    cotangent,
):
    rows_in, cols_in, in_width = input_field.shape
    rows_dev = rows_in // 2
    cols_dev = cols_in // 2
    basis_count = encoder_filter.shape[1]
    tap_count = encoder_filter.shape[2]
    channels = block_weights.shape[2]
    layers = block_weights.shape[0]
    cell_count = rows_dev * cols_dev
    extended_in = padded(input_field, (("lon", 1),), TAP_REACH, True)
    filter_values = encoder_filter.astype(jnp.float32)
    accumulated = jnp.zeros((rows_in, cols_dev, basis_count, in_width), jnp.float32)
    for tap_index in range(tap_count):
        sampled = extended_in[:, tap_index : tap_index + cols_in : 2, :]
        accumulated = (
            accumulated
            + sampled[:, :, None, :].astype(jnp.float32)
            * filter_values[:, None, :, tap_index, None]
        )
    filtered_in = accumulated.astype(jnp.bfloat16).reshape(
        rows_in, cols_dev * basis_count * in_width
    )
    first_row = lax.axis_index(("lat", "ch")) * rows_dev
    relative = row_owner - first_row + 1
    selector = (relative[None, :] == jnp.arange(rows_dev + 2, dtype=jnp.int32)[:, None]).astype(
        jnp.bfloat16
    )
    summed = jnp.dot(selector, filtered_in, preferred_element_type=jnp.float32)
    from_above = from_behind(summed[0:1].astype(jnp.bfloat16), ("lat", "ch"), -1).astype(
        jnp.float32
    )
    from_below = from_behind(summed[rows_dev + 1 :].astype(jnp.bfloat16), ("lat", "ch"), 1).astype(
        jnp.float32
    )
    regridded = add_edges(summed[1 : rows_dev + 1], from_below, from_above)
    latent_in = regridded.astype(jnp.bfloat16).reshape(cell_count, basis_count * in_width)
    current = jnp.dot(latent_in, encoder_weight, preferred_element_type=jnp.float32).astype(
        jnp.bfloat16
    )
    current = current.reshape(rows_dev, cols_dev, channels)
    offsets = jnp.abs(jnp.arange(2 * REACH + 1, dtype=jnp.int32) - REACH)
    keep = offsets[None, :] <= row_widths[:, None]
    masked = jnp.where(keep[:, None, None, :], disco_basis, jnp.zeros_like(disco_basis))
    ext_cols = cols_dev + 2 * REACH
    differences = (
        jnp.arange(ext_cols, dtype=jnp.int32)[None, :]
        - jnp.arange(cols_dev, dtype=jnp.int32)[:, None]
    )
    placement = (
        differences[:, :, None] == jnp.arange(2 * REACH + 1, dtype=jnp.int32)[None, None, :]
    ).astype(jnp.bfloat16)
    banded = jnp.einsum(
        "ikrt,jqt->ikrjq", masked, placement, preferred_element_type=jnp.float32
    ).astype(jnp.bfloat16)
    saved = []
    for layer_index in range(layers):
        rows_ext = padded(current, ((("lat", "ch"), 0),), 1, False)
        extended = padded(rows_ext, (("lon", 1),), REACH, True)
        features = (
            apply_basis(banded, extended, rows_dev)
            .astype(jnp.bfloat16)
            .reshape(cell_count, basis_count * channels)
        )
        preact = jnp.dot(features, block_weights[layer_index], preferred_element_type=jnp.float32)
        current = (
            current.astype(jnp.float32) + jax.nn.silu(preact).reshape(rows_dev, cols_dev, channels)
        ).astype(jnp.bfloat16)
        saved.append((features, preact))
    gradient = cotangent
    weight_terms = [None] * layers
    for layer_index in reversed(range(layers)):
        features, preact = saved[layer_index]
        sigma = jax.nn.sigmoid(preact)
        upstream = gradient.reshape(cell_count, channels).astype(jnp.float32)
        act_grad = (upstream * sigma * (1.0 + preact * (1.0 - sigma))).astype(jnp.bfloat16)
        weight_terms[layer_index] = lax.dot_general(
            features, act_grad, (((0,), (0,)), ((), ())), preferred_element_type=jnp.float32
        )
        errors = lax.dot_general(
            act_grad,
            block_weights[layer_index],
            (((1,), (1,)), ((), ())),
            preferred_element_type=jnp.float32,
        )
        errors = errors.astype(jnp.bfloat16).reshape(rows_dev, cols_dev, basis_count, channels)
        spread = spread_basis(banded, errors)
        returned = return_rims(spread, cols_dev)
        gradient = (gradient.astype(jnp.float32) + returned).astype(jnp.bfloat16)
    encoder_term = lax.dot_general(
        latent_in,
        gradient.reshape(cell_count, channels),
        (((0,), (0,)), ((), ())),
        preferred_element_type=jnp.float32,
    )
    block_stack = jnp.concatenate(weight_terms, axis=0)
    own_width = channels // lax.axis_size("ch")
    block_part, encoder_part = (
        lax.psum_scatter(
            block_stack.astype(jnp.bfloat16), "ch", scatter_dimension=1, tiled=True
        ).astype(jnp.float32),
        lax.psum_scatter(
            encoder_term.astype(jnp.bfloat16), "ch", scatter_dimension=1, tiled=True
        ).astype(jnp.float32),
    )
    block_sum, encoder_sum = lax.psum((block_part, encoder_part), ("lon", "lat"))
    cells_total = cell_count * lax.axis_size("lon") * lax.axis_size(("lat", "ch"))
    normalizer = 1.0 / math.sqrt(cells_total)
    block_grads = (block_sum * normalizer).reshape(layers, basis_count * channels, own_width)
    encoder_grad = encoder_sum * normalizer
    return (current, gradient, block_grads, encoder_grad)


def solution(mesh):
    placed = (
        P(("ens", "lat", "ch"), "lon", None),
        P(("lat", "ch"), None, None),
        P(("ens", "lat", "ch")),
        P(),
        P(("lat", "ch"), None, None, None),
        P(("lat", "ch")),
        P(),
        P(("ens", "lat", "ch"), "lon", None),
    )
    return jax.shard_map(
        per_device,
        mesh=mesh,
        in_specs=placed,
        out_specs=(
            P(("ens", "lat", "ch"), "lon", None),
            P(("ens", "lat", "ch"), "lon", None),
            P("ens", None, "ch"),
            P("ens", "ch"),
        ),
        check_vma=False,
    )
```

profile of v0, /device:TPU:0, one launch (start us, length us, event | category | flops | bytes accessed | tf_op | source)
XLA Modules:
  0.0 203.9 jit_solution(1901425106041720855)
XLA Ops:
  7.2 1.0 fusion.64
  8.2 3.1 %collective-permute-start = (bf16[32,2,128]{2,1,0:T(2,128)(2,1)S(1)}, bf16[32,2,128]{2,1,0:T(2,128)(2,1)S(1)}, u32[]{:S(2)}, u32[]{:S(2)}) collective-permute-start(bf16[32,2,128]{2,1,0:T(2,128)(2,1)S(1)} %get-tuple-element.25), channel_id=1, source_target_pairs={{0,4},{4,8},{8,12},{12,0},{1,5},{5,9},{9,13},{13,1},{2,6},{6,10},{... | collective-permute-start | bytes 49160 | tf_op jit(solution)/shard_map/ppermute | solution.py:31
  11.3 2.1 %collective-permute-start.1 = (bf16[32,2,128]{2,1,0:T(2,128)(2,1)S(1)}, bf16[32,2,128]{2,1,0:T(2,128)(2,1)S(1)}, u32[]{:S(2)}, u32[]{:S(2)}) collective-permute-start(bf16[32,2,128]{2,1,0:T(2,128)(2,1)S(1)} %get-tuple-element.26), channel_id=1, source_target_pairs={{4,0},{8,4},{12,8},{0,12},{5,1},{9,5},{13,9},{1,13},{6,2},{10,6},{... | collective-permute-start | bytes 49160 | tf_op jit(solution)/shard_map/ppermute | solution.py:34
  14.1 0.7 broadcast_compare_fusion
  14.8 0.8 select_bitcast_fusion
  16.3 1.8 slice.167
  20.8 1.0 add_convert_fusion
  22.5 1.5 collective-permute-start.2
  24.0 1.3 collective-permute-start.3
  25.3 3.5 %collective-permute-done.3 = bf16[1,8192]{1,0:T(2,128)(2,1)S(1)} collective-permute-done((bf16[1,8192]{1,0:T(2,128)(2,1)S(1)}, bf16[1,8192]{1,0:T(2,128)(2,1)S(1)}, u32[]{:S(2)}, u32[]{:S(2)}) %collective-permute-start.3) | collective-permute-done | bytes 16416 | tf_op jit(solution)/shard_map/ppermute | solution.py:21
  29.3 4.5 %collective-permute-start.4 = (bf16[1,16,256]{2,1,0:T(8,128)(2,1)S(1)}, bf16[1,16,256]{2,1,0:T(8,128)(2,1)S(1)}, u32[]{:S(2)}, u32[]{:S(2)}) collective-permute-start(bf16[1,16,256]{2,1,0:T(8,128)(2,1)S(1)} %get-tuple-element.33), channel_id=1, source_target_pairs={{0,1},{1,2},{2,3},{4,5},{5,6},{6,7},{8,9},{9,10},{10,11},{12,13},{... | collective-permute-start | bytes 24584 | tf_op jit(solution)/shard_map/ppermute | solution.py:31
  33.9 1.3 collective-permute-start.5
  35.6 1.4 collective-permute-done.5
  37.1 3.8 %collective-permute-start.7 = (bf16[18,8,256]{2,1,0:T(8,128)(2,1)S(1)}, bf16[18,8,256]{2,1,0:T(8,128)(2,1)S(1)}, u32[]{:S(2)}, u32[]{:S(2)}) collective-permute-start(bf16[18,8,256]{2,1,0:T(8,128)(2,1)S(1)} %get-tuple-element.30), channel_id=1, source_target_pairs={{4,0},{8,4},{12,8},{0,12},{5,1},{9,5},{13,9},{1,13},{6,2},{10,6},{... | collective-permute-start | bytes 221192 | tf_op jit(solution)/shard_map/ppermute | solution.py:34
  41.0 2.3 %collective-permute-done.6 = bf16[18,8,256]{2,1,0:T(8,128)(2,1)S(1)} collective-permute-done((bf16[18,8,256]{2,1,0:T(8,128)(2,1)S(1)}, bf16[18,8,256]{2,1,0:T(8,128)(2,1)S(1)}, u32[]{:S(2)}, u32[]{:S(2)}) %collective-permute-start.6) | collective-permute-done | bytes 73760 | tf_op jit(solution)/shard_map/ppermute | solution.py:31
  44.6 0.8 copy-done.1
  45.4 1.0 fusion.37
  46.5 3.2 %collective-permute-start.8 = (bf16[1,16,256]{2,1,0:T(8,128)(2,1)S(1)}, bf16[1,16,256]{2,1,0:T(8,128)(2,1)S(1)}, u32[]{:S(2)}, u32[]{:S(2)}) collective-permute-start(bf16[1,16,256]{2,1,0:T(8,128)(2,1)S(1)} %get-tuple-element.31), channel_id=1, source_target_pairs={{0,1},{1,2},{2,3},{4,5},{5,6},{6,7},{8,9},{9,10},{10,11},{12,13},{... | collective-permute-start | bytes 24584 | tf_op jit(solution)/shard_map/ppermute | solution.py:31
  49.7 1.3 collective-permute-start.9
  51.0 1.8 collective-permute-done.9
  52.9 3.9 %collective-permute-start.11 = (bf16[18,8,256]{2,1,0:T(8,128)(2,1)S(1)}, bf16[18,8,256]{2,1,0:T(8,128)(2,1)S(1)}, u32[]{:S(2)}, u32[]{:S(2)}) collective-permute-start(bf16[18,8,256]{2,1,0:T(8,128)(2,1)S(1)} %get-tuple-element.28), channel_id=1, source_target_pairs={{4,0},{8,4},{12,8},{0,12},{5,1},{9,5},{13,9},{1,13},{6,2},{10,6},{... | collective-permute-start | bytes 221192 | tf_op jit(solution)/shard_map/ppermute | solution.py:34
  56.8 2.4 %collective-permute-done.10 = bf16[18,8,256]{2,1,0:T(8,128)(2,1)S(1)} collective-permute-done((bf16[18,8,256]{2,1,0:T(8,128)(2,1)S(1)}, bf16[18,8,256]{2,1,0:T(8,128)(2,1)S(1)}, u32[]{:S(2)}, u32[]{:S(2)}) %collective-permute-start.10) | collective-permute-done | bytes 73760 | tf_op jit(solution)/shard_map/ppermute | solution.py:31
  61.0 1.1 fusion.35
  64.5 1.3 collective-permute-start.12
  65.8 2.7 %collective-permute-start.13 = (bf16[18,8,256]{2,1,0:T(8,128)(2,1)S(1)}, bf16[18,8,256]{2,1,0:T(8,128)(2,1)S(1)}, u32[]{:S(2)}, u32[]{:S(2)}) collective-permute-start(bf16[18,8,256]{2,1,0:T(8,128)(2,1)S(1)} %get-tuple-element.22), channel_id=1, source_target_pairs={{0,12},{4,0},{8,4},{12,8},{1,13},{5,1},{9,5},{13,9},{2,14},{6,2},{... | collective-permute-start | bytes 221192 | tf_op jit(solution)/shard_map/ppermute | solution.py:15
  68.5 2.4 %collective-permute-done.12 = bf16[18,8,256]{2,1,0:T(8,128)(2,1)S(1)} collective-permute-done((bf16[18,8,256]{2,1,0:T(8,128)(2,1)S(1)}, bf16[18,8,256]{2,1,0:T(8,128)(2,1)S(1)}, u32[]{:S(2)}, u32[]{:S(2)}) %collective-permute-start.12) | collective-permute-done | bytes 73760 | tf_op jit(solution)/shard_map/ppermute | solution.py:15
  70.9 1.9 collective-permute-done.13
  72.9 2.1 %collective-permute-start.14 = (f32[1,16,256]{2,1,0:T(8,128)S(1)}, f32[1,16,256]{2,1,0:T(8,128)S(1)}, u32[]{:S(2)}, u32[]{:S(2)}) collective-permute-start(f32[1,16,256]{2,1,0:T(8,128)S(1)} %get-tuple-element.19), channel_id=1, source_target_pairs={{0,1},{1,2},{2,3},{4,5},{5,6},{6,7},{8,9},{9,10},{10,11},{12,13},{... | collective-permute-start | bytes 49160 | tf_op jit(solution)/shard_map/ppermute | solution.py:21
  74.9 1.3 collective-permute-start.15
  76.2 1.8 collective-permute-done.15
  78.2 1.1 convolution_convert_fusion.3
  79.4 1.4 reshape.128
  81.8 1.1 collective-permute-start.16
  83.0 2.8 %collective-permute-start.17 = (bf16[18,8,256]{2,1,0:T(8,128)(2,1)S(1)}, bf16[18,8,256]{2,1,0:T(8,128)(2,1)S(1)}, u32[]{:S(2)}, u32[]{:S(2)}) collective-permute-start(bf16[18,8,256]{2,1,0:T(8,128)(2,1)S(1)} %get-tuple-element.18), channel_id=1, source_target_pairs={{0,12},{4,0},{8,4},{12,8},{1,13},{5,1},{9,5},{13,9},{2,14},{6,2},{... | collective-permute-start | bytes 221192 | tf_op jit(solution)/shard_map/ppermute | solution.py:15
  85.7 2.4 %collective-permute-done.16 = bf16[18,8,256]{2,1,0:T(8,128)(2,1)S(1)} collective-permute-done((bf16[18,8,256]{2,1,0:T(8,128)(2,1)S(1)}, bf16[18,8,256]{2,1,0:T(8,128)(2,1)S(1)}, u32[]{:S(2)}, u32[]{:S(2)}) %collective-permute-start.16) | collective-permute-done | bytes 73760 | tf_op jit(solution)/shard_map/ppermute | solution.py:15
  88.2 3.7 %collective-permute-start.18 = (f32[1,16,256]{2,1,0:T(8,128)S(1)}, f32[1,16,256]{2,1,0:T(8,128)S(1)}, u32[]{:S(2)}, u32[]{:S(2)}) collective-permute-start(f32[1,16,256]{2,1,0:T(8,128)S(1)} %get-tuple-element.15), channel_id=1, source_target_pairs={{0,1},{1,2},{2,3},{4,5},{5,6},{6,7},{8,9},{9,10},{10,11},{12,13},{... | collective-permute-start | bytes 49160 | tf_op jit(solution)/shard_map/ppermute | solution.py:21
  92.0 1.4 collective-permute-start.19
  93.4 1.9 collective-permute-done.19
  95.6 0.8 copy.106
  97.4 1.4 copy.104
  98.8 0.9 copy-done.7
  100.4 6.6 %reduce-scatter.9.cloned.1.call-done = bf16[128,512]{1,0:T(8,128)(2,1)} async-done(((bf16[256,512]{1,0:T(8,128)(2,1)}), bf16[128,512]{1,0:T(8,128)(2,1)}) %reduce-scatter.9.cloned.1.call-update) | async-done | bytes 131088
  107.0 1.0 copy.107
  108.0 11.3 %reduce-scatter.7.cloned.1.call-done = bf16[128,2048]{1,0:T(8,128)(2,1)} async-done(((bf16[256,2048]{1,0:T(8,128)(2,1)}), bf16[128,2048]{1,0:T(8,128)(2,1)}) %reduce-scatter.7.cloned.1.call-update) | async-done | bytes 524304
  119.3 1.3 copy.105
  120.6 74.7 %all-reduce.18 = (f32[2048,128]{1,0:T(8,128)S(1)}, f32[512,128]{1,0:T(8,128)S(1)}) all-reduce(bf16[2048,128]{1,0:T(8,128)(2,1)S(1)} %copy.105, bf16[512,128]{1,0:T(8,128)(2,1)S(1)} %copy.107), channel_id=1, replica_groups=mesh['ens'=2,'lon'=4,'lat'=2,'ch'=2] {'lon','lat'}, use_global_device_ids=true, to_apply=%region_1.2 | all-reduce | flops 327680 | bytes 1966080 | tf_op jit(solution)/shard_map/psum | solution.py:200
  195.3 1.0 broadcast_multiply_fusion
  196.4 0.7 broadcast_multiply_fusion.1
  (107 shorter events, 14.3 us)
Async XLA Ops:
  7.2 21.9 %copy-start = (bf16[512,256]{1,0:T(8,128)(2,1)S(1)}, bf16[512,256]{1,0:T(8,128)(2,1)}, u32[]{:S(2)}) copy-start(bf16[512,256]{1,0:T(8,128)(2,1)} %param.11) | copy-start | bytes 786436
  7.2 11.5 %copy-start.3 = (bf16[32,32,128]{2,1,0:T(8,128)(2,1)S(1)}, bf16[32,32,128]{2,1,0:T(8,128)(2,1)}, u32[]{:S(2)}) copy-start(bf16[32,32,128]{2,1,0:T(8,128)(2,1)} %param.8) | copy-start | bytes 786436
  7.2 99.8 %reduce-scatter.9.cloned.1.call-start = ((), (), s32[]{:S(2)}) async-start(), calls=%async_computation.3 | async-start | bytes 393216
  8.2 10.4 %collective-permute-start = (bf16[32,2,128]{2,1,0:T(2,128)(2,1)S(1)}, bf16[32,2,128]{2,1,0:T(2,128)(2,1)S(1)}, u32[]{:S(2)}, u32[]{:S(2)}) collective-permute-start(bf16[32,2,128]{2,1,0:T(2,128)(2,1)S(1)} %get-tuple-element.25), channel_id=1, source_target_pairs={{0,4},{4,8},{8,12},{12,0},{1,5},{5,9},{9,13},{13,1},{2,6},{6,10},{... | collective-permute-start | bytes 49160 | tf_op jit(solution)/shard_map/ppermute | solution.py:31
  11.3 7.3 %collective-permute-start.1 = (bf16[32,2,128]{2,1,0:T(2,128)(2,1)S(1)}, bf16[32,2,128]{2,1,0:T(2,128)(2,1)S(1)}, u32[]{:S(2)}, u32[]{:S(2)}) collective-permute-start(bf16[32,2,128]{2,1,0:T(2,128)(2,1)S(1)} %get-tuple-element.26), channel_id=1, source_target_pairs={{4,0},{8,4},{12,8},{0,12},{5,1},{9,5},{13,9},{1,13},{6,2},{10,6},{... | collective-permute-start | bytes 49160 | tf_op jit(solution)/shard_map/ppermute | solution.py:34
  22.5 2.8 %collective-permute-start.2 = (bf16[1,8192]{1,0:T(2,128)(2,1)S(1)}, bf16[1,8192]{1,0:T(2,128)(2,1)S(1)}, u32[]{:S(2)}, u32[]{:S(2)}) collective-permute-start(bf16[1,8192]{1,0:T(2,128)(2,1)S(1)} %get-tuple-element.13), channel_id=1, source_target_pairs={{0,1},{1,2},{2,3},{4,5},{5,6},{6,7},{8,9},{9,10},{10,11},{12,13},{... | collective-permute-start | bytes 49160 | tf_op jit(solution)/shard_map/ppermute | solution.py:21
  24.0 4.8 %collective-permute-start.3 = (bf16[1,8192]{1,0:T(2,128)(2,1)S(1)}, bf16[1,8192]{1,0:T(2,128)(2,1)S(1)}, u32[]{:S(2)}, u32[]{:S(2)}) collective-permute-start(bf16[1,8192]{1,0:T(2,128)(2,1)S(1)} %get-tuple-element.14), channel_id=1, source_target_pairs={{1,0},{2,1},{3,2},{5,4},{6,5},{7,6},{9,8},{10,9},{11,10},{13,12},{... | collective-permute-start | bytes 49160 | tf_op jit(solution)/shard_map/ppermute | solution.py:21
  29.3 6.2 %collective-permute-start.4 = (bf16[1,16,256]{2,1,0:T(8,128)(2,1)S(1)}, bf16[1,16,256]{2,1,0:T(8,128)(2,1)S(1)}, u32[]{:S(2)}, u32[]{:S(2)}) collective-permute-start(bf16[1,16,256]{2,1,0:T(8,128)(2,1)S(1)} %get-tuple-element.33), channel_id=1, source_target_pairs={{0,1},{1,2},{2,3},{4,5},{5,6},{6,7},{8,9},{9,10},{10,11},{12,13},{... | collective-permute-start | bytes 24584 | tf_op jit(solution)/shard_map/ppermute | solution.py:31
  33.9 3.1 %collective-permute-start.5 = (bf16[1,16,256]{2,1,0:T(8,128)(2,1)S(1)}, bf16[1,16,256]{2,1,0:T(8,128)(2,1)S(1)}, u32[]{:S(2)}, u32[]{:S(2)}) collective-permute-start(bf16[1,16,256]{2,1,0:T(8,128)(2,1)S(1)} %get-tuple-element.34), channel_id=1, source_target_pairs={{1,0},{2,1},{3,2},{5,4},{6,5},{7,6},{9,8},{10,9},{11,10},{13,12},{... | collective-permute-start | bytes 24584 | tf_op jit(solution)/shard_map/ppermute | solution.py:34
  37.0 6.3 %collective-permute-start.6 = (bf16[18,8,256]{2,1,0:T(8,128)(2,1)S(1)}, bf16[18,8,256]{2,1,0:T(8,128)(2,1)S(1)}, u32[]{:S(2)}, u32[]{:S(2)}) collective-permute-start(bf16[18,8,256]{2,1,0:T(8,128)(2,1)S(1)} %get-tuple-element.29), channel_id=1, source_target_pairs={{0,4},{4,8},{8,12},{12,0},{1,5},{5,9},{9,13},{13,1},{2,6},{6,10},{... | collective-permute-start | bytes 221192 | tf_op jit(solution)/shard_map/ppermute | solution.py:31
  37.1 6.2 %collective-permute-start.7 = (bf16[18,8,256]{2,1,0:T(8,128)(2,1)S(1)}, bf16[18,8,256]{2,1,0:T(8,128)(2,1)S(1)}, u32[]{:S(2)}, u32[]{:S(2)}) collective-permute-start(bf16[18,8,256]{2,1,0:T(8,128)(2,1)S(1)} %get-tuple-element.30), channel_id=1, source_target_pairs={{4,0},{8,4},{12,8},{0,12},{5,1},{9,5},{13,9},{1,13},{6,2},{10,6},{... | collective-permute-start | bytes 221192 | tf_op jit(solution)/shard_map/ppermute | solution.py:34
  44.2 1.2 copy-start.1
  46.5 4.5 %collective-permute-start.8 = (bf16[1,16,256]{2,1,0:T(8,128)(2,1)S(1)}, bf16[1,16,256]{2,1,0:T(8,128)(2,1)S(1)}, u32[]{:S(2)}, u32[]{:S(2)}) collective-permute-start(bf16[1,16,256]{2,1,0:T(8,128)(2,1)S(1)} %get-tuple-element.31), channel_id=1, source_target_pairs={{0,1},{1,2},{2,3},{4,5},{5,6},{6,7},{8,9},{9,10},{10,11},{12,13},{... | collective-permute-start | bytes 24584 | tf_op jit(solution)/shard_map/ppermute | solution.py:31
  49.7 3.1 %collective-permute-start.9 = (bf16[1,16,256]{2,1,0:T(8,128)(2,1)S(1)}, bf16[1,16,256]{2,1,0:T(8,128)(2,1)S(1)}, u32[]{:S(2)}, u32[]{:S(2)}) collective-permute-start(bf16[1,16,256]{2,1,0:T(8,128)(2,1)S(1)} %get-tuple-element.32), channel_id=1, source_target_pairs={{1,0},{2,1},{3,2},{5,4},{6,5},{7,6},{9,8},{10,9},{11,10},{13,12},{... | collective-permute-start | bytes 24584 | tf_op jit(solution)/shard_map/ppermute | solution.py:34
  52.9 6.3 %collective-permute-start.10 = (bf16[18,8,256]{2,1,0:T(8,128)(2,1)S(1)}, bf16[18,8,256]{2,1,0:T(8,128)(2,1)S(1)}, u32[]{:S(2)}, u32[]{:S(2)}) collective-permute-start(bf16[18,8,256]{2,1,0:T(8,128)(2,1)S(1)} %get-tuple-element.27), channel_id=1, source_target_pairs={{0,4},{4,8},{8,12},{12,0},{1,5},{5,9},{9,13},{13,1},{2,6},{6,10},{... | collective-permute-start | bytes 221192 | tf_op jit(solution)/shard_map/ppermute | solution.py:31
  52.9 6.2 %collective-permute-start.11 = (bf16[18,8,256]{2,1,0:T(8,128)(2,1)S(1)}, bf16[18,8,256]{2,1,0:T(8,128)(2,1)S(1)}, u32[]{:S(2)}, u32[]{:S(2)}) collective-permute-start(bf16[18,8,256]{2,1,0:T(8,128)(2,1)S(1)} %get-tuple-element.28), channel_id=1, source_target_pairs={{4,0},{8,4},{12,8},{0,12},{5,1},{9,5},{13,9},{1,13},{6,2},{10,6},{... | collective-permute-start | bytes 221192 | tf_op jit(solution)/shard_map/ppermute | solution.py:34
  60.1 0.9 copy-start.9
  62.1 0.7 copy-start.4
  64.5 13.6 %copy-start.10 = (bf16[16,16,256]{2,1,0:T(8,128)(2,1)S(1)}, bf16[16,16,256]{2,1,0:T(8,128)(2,1)}, u32[]{:S(2)}) copy-start(bf16[16,16,256]{2,1,0:T(8,128)(2,1)} %param.15) | copy-start | bytes 393220
  64.5 13.6 %copy-start.8 = (f32[256,256]{1,0:T(8,128)S(1)}, f32[256,256]{1,0:T(8,128)}, u32[]{:S(2)}) copy-start(f32[256,256]{1,0:T(8,128)} %get-tuple-element.43) | copy-start | bytes 786436
  64.5 6.4 %collective-permute-start.12 = (bf16[18,8,256]{2,1,0:T(8,128)(2,1)S(1)}, bf16[18,8,256]{2,1,0:T(8,128)(2,1)S(1)}, u32[]{:S(2)}, u32[]{:S(2)}) collective-permute-start(bf16[18,8,256]{2,1,0:T(8,128)(2,1)S(1)} %get-tuple-element.21), channel_id=1, source_target_pairs={{0,4},{4,8},{8,12},{12,0},{1,5},{5,9},{9,13},{13,1},{2,6},{6,10},{... | collective-permute-start | bytes 221192 | tf_op jit(solution)/shard_map/ppermute | solution.py:15
  65.8 7.0 %collective-permute-start.13 = (bf16[18,8,256]{2,1,0:T(8,128)(2,1)S(1)}, bf16[18,8,256]{2,1,0:T(8,128)(2,1)S(1)}, u32[]{:S(2)}, u32[]{:S(2)}) collective-permute-start(bf16[18,8,256]{2,1,0:T(8,128)(2,1)S(1)} %get-tuple-element.22), channel_id=1, source_target_pairs={{0,12},{4,0},{8,4},{12,8},{1,13},{5,1},{9,5},{13,9},{2,14},{6,2},{... | collective-permute-start | bytes 221192 | tf_op jit(solution)/shard_map/ppermute | solution.py:15
  72.8 5.4 %copy-start.2 = (bf16[2,1024,256]{2,1,0:T(8,128)(2,1)S(1)}, bf16[2,1024,256]{2,1,0:T(8,128)(2,1)}, u32[]{:S(2)}) copy-start(bf16[2,1024,256]{2,1,0:T(8,128)(2,1)} %param.14) | copy-start | bytes 3145732
  72.9 3.4 %collective-permute-start.14 = (f32[1,16,256]{2,1,0:T(8,128)S(1)}, f32[1,16,256]{2,1,0:T(8,128)S(1)}, u32[]{:S(2)}, u32[]{:S(2)}) collective-permute-start(f32[1,16,256]{2,1,0:T(8,128)S(1)} %get-tuple-element.19), channel_id=1, source_target_pairs={{0,1},{1,2},{2,3},{4,5},{5,6},{6,7},{8,9},{9,10},{10,11},{12,13},{... | collective-permute-start | bytes 49160 | tf_op jit(solution)/shard_map/ppermute | solution.py:21
  74.9 3.1 %collective-permute-start.15 = (f32[1,16,256]{2,1,0:T(8,128)S(1)}, f32[1,16,256]{2,1,0:T(8,128)S(1)}, u32[]{:S(2)}, u32[]{:S(2)}) collective-permute-start(f32[1,16,256]{2,1,0:T(8,128)S(1)} %get-tuple-element.20), channel_id=1, source_target_pairs={{1,0},{2,1},{3,2},{5,4},{6,5},{7,6},{9,8},{10,9},{11,10},{13,12},{... | collective-permute-start | bytes 49160 | tf_op jit(solution)/shard_map/ppermute | solution.py:21
  81.8 6.3 %collective-permute-start.16 = (bf16[18,8,256]{2,1,0:T(8,128)(2,1)S(1)}, bf16[18,8,256]{2,1,0:T(8,128)(2,1)S(1)}, u32[]{:S(2)}, u32[]{:S(2)}) collective-permute-start(bf16[18,8,256]{2,1,0:T(8,128)(2,1)S(1)} %get-tuple-element.17), channel_id=1, source_target_pairs={{0,4},{4,8},{8,12},{12,0},{1,5},{5,9},{9,13},{13,1},{2,6},{6,10},{... | collective-permute-start | bytes 221192 | tf_op jit(solution)/shard_map/ppermute | solution.py:15
  83.0 5.2 %collective-permute-start.17 = (bf16[18,8,256]{2,1,0:T(8,128)(2,1)S(1)}, bf16[18,8,256]{2,1,0:T(8,128)(2,1)S(1)}, u32[]{:S(2)}, u32[]{:S(2)}) collective-permute-start(bf16[18,8,256]{2,1,0:T(8,128)(2,1)S(1)} %get-tuple-element.18), channel_id=1, source_target_pairs={{0,12},{4,0},{8,4},{12,8},{1,13},{5,1},{9,5},{13,9},{2,14},{6,2},{... | collective-permute-start | bytes 221192 | tf_op jit(solution)/shard_map/ppermute | solution.py:15
  88.2 5.2 %collective-permute-start.18 = (f32[1,16,256]{2,1,0:T(8,128)S(1)}, f32[1,16,256]{2,1,0:T(8,128)S(1)}, u32[]{:S(2)}, u32[]{:S(2)}) collective-permute-start(f32[1,16,256]{2,1,0:T(8,128)S(1)} %get-tuple-element.15), channel_id=1, source_target_pairs={{0,1},{1,2},{2,3},{4,5},{5,6},{6,7},{8,9},{9,10},{10,11},{12,13},{... | collective-permute-start | bytes 49160 | tf_op jit(solution)/shard_map/ppermute | solution.py:21
  91.9 4.6 %copy-start.5 = (bf16[256,256]{1,0:T(8,128)(2,1)S(1)}, bf16[256,256]{1,0:T(8,128)(2,1)}, u32[]{:S(2)}) copy-start(bf16[256,256]{1,0:T(8,128)(2,1)} %copy-done.4) | copy-start | bytes 393220
  92.0 3.3 %collective-permute-start.19 = (f32[1,16,256]{2,1,0:T(8,128)S(1)}, f32[1,16,256]{2,1,0:T(8,128)S(1)}, u32[]{:S(2)}, u32[]{:S(2)}) collective-permute-start(f32[1,16,256]{2,1,0:T(8,128)S(1)} %get-tuple-element.16), channel_id=1, source_target_pairs={{1,0},{2,1},{3,2},{5,4},{6,5},{7,6},{9,8},{10,9},{11,10},{13,12},{... | collective-permute-start | bytes 49160 | tf_op jit(solution)/shard_map/ppermute | solution.py:21
  95.3 1.6 copy-start.6
  96.5 22.8 %reduce-scatter.7.cloned.1.call-start = ((), (), s32[]{:S(2)}) async-start(), calls=%async_computation.2 | async-start | bytes 1572864
  98.8 0.9 copy-start.7
Sparse Core Ops, SparseCore 0:
  96.6 10.3 reduce-scatter.8
  109.8 9.4 reduce-scatter.6
where the time goes:
time: 205 us; the launch traced here: 204 us
  blocking collectives  74.7 us (36%)
  starting transfers between devices  42.6 us (21%)
  waiting for transfers between devices  39.8 us (19%)
  local copies, waits for them, and re-layouts  15.9 us (8%)
  between operations  14.7 us (7%)
  matrix products  8.68 us (4%)
  other arithmetic  7.58 us (4%)
    psum x1, blocking collectives, per_device(): lax.psum((block_part, encoder_part), ('lon', 'lat'))  74.7 us
    unnamed x4, waiting for transfers between devices  17.9 us
    ppermute x5, starting transfers between devices, padded(): lax.ppermute(lax.slice_in_dim(block, 0, width, axis=dim), axis, backward)  12.4 us
    ppermute x6, starting transfers between devices, from_behind(): return lax.ppermute(block, axis, route)  11.3 us
    ppermute x5, starting transfers between devices, padded(): lax.ppermute(lax.slice_in_dim(block, block.shape[dim] - width, None, axis...  11 us
    ppermute x4, starting transfers between devices, passed_along(): return lax.ppermute(value, axis, pairs)  7.87 us
    unnamed x28, local copies, waits for them, and re-layouts  7.76 us
    ppermute x6, waiting for transfers between devices, from_behind(): return lax.ppermute(block, axis, route)  7.23 us
  transfers between devices with their start and end apart: 22, of which 12 were waited for; matrix products, arithmetic and copies ran while one was open for 5% of the time, Pallas kernels for 0%

commit v1 on v0

--- a/solution.py
+++ b/solution.py
@@ -1,12 +1,156 @@
+import functools
 import math
 
 import jax
 import jax.numpy as jnp
 from jax import lax
+from jax.experimental import pallas as pl
+from jax.experimental.pallas import tpu as pltpu
 from jax.sharding import PartitionSpec as P
 
 REACH = 8
 TAP_REACH = 2
+MESH = pl.DeviceIdType.MESH
+
+
+class GradSum:
+    def __init__(self, sizes, source, result, bufs, sems):
+        self.lon, self.lat = sizes
+        self.source, self.result = source, result
+        self.rec_ch, self.part, self.rec_lon, self.piece, self.rec_lat, self.whole = bufs
+        self.ssem, self.rsem = sems
+        self.rows = part_rows = self.part.shape[0]
+        self.span = part_rows // self.lon
+        self.width = self.part.shape[1]
+        self.my_lon = lax.axis_index("lon")
+        self.my_lat = lax.axis_index("lat")
+        self.my_ch = lax.axis_index("ch")
+        self.pending = []
+
+    @staticmethod
+    def scratch(sizes, rows, width):
+        lon, lat = sizes
+        span = rows // lon
+        count = 1 + 2 * (lon - 1) + (lat - 1)
+        return [
+            pltpu.VMEM((rows, width), jnp.bfloat16),
+            pltpu.VMEM((rows, width), jnp.bfloat16),
+            pltpu.VMEM((lon - 1, span, width), jnp.bfloat16),
+            pltpu.VMEM((span, width), jnp.bfloat16),
+            pltpu.VMEM((lat - 1, span, width), jnp.bfloat16),
+            pltpu.VMEM((span, width), jnp.bfloat16),
+            pltpu.SemaphoreType.DMA((count,)),
+            pltpu.SemaphoreType.DMA((count,)),
+        ]
+
+    def send(self, source, target, slot, device):
+        copy = pltpu.make_async_remote_copy(
+            src_ref=source,
+            dst_ref=target,
+            send_sem=self.ssem.at[slot],
+            recv_sem=self.rsem.at[slot],
+            device_id=device,
+            device_id_type=MESH,
+        )
+        copy.start()
+        self.pending.append(copy)
+
+    def settle(self):
+        for copy in self.pending:
+            copy.wait()
+        self.pending = []
+
+    def columns(self, half):
+        return pl.ds(pl.multiple_of(half * self.width, self.width), self.width)
+
+    def stretch(self, owner):
+        return pl.ds(pl.multiple_of(owner * self.span, self.span), self.span)
+
+    def start_ch(self):
+        other = 1 - self.my_ch
+        self.send(self.source.at[:, self.columns(other)], self.rec_ch, 0, {"ch": other})
+
+    def start_lon(self):
+        self.settle()
+        own = self.source[:, self.columns(self.my_ch)].astype(jnp.float32)
+        self.part[...] = (own + self.rec_ch[...].astype(jnp.float32)).astype(jnp.bfloat16)
+        for step in range(1, self.lon):
+            peer = lax.rem(self.my_lon + step, self.lon)
+            self.send(
+                self.part.at[self.stretch(peer)], self.rec_lon.at[step - 1], step, {"lon": peer}
+            )
+
+    def start_lat(self):
+        self.settle()
+        total = self.part[self.stretch(self.my_lon), :].astype(jnp.float32)
+        for step in range(1, self.lon):
+            total = total + self.rec_lon[step - 1].astype(jnp.float32)
+        self.piece[...] = total.astype(jnp.bfloat16)
+        for step in range(1, self.lat):
+            peer = lax.rem(self.my_lat + step, self.lat)
+            self.send(self.piece, self.rec_lat.at[step - 1], self.lon + step - 1, {"lat": peer})
+
+    def start_gather(self):
+        self.settle()
+        total = self.piece[...].astype(jnp.float32)
+        for step in range(1, self.lat):
+            total = total + self.rec_lat[step - 1].astype(jnp.float32)
+        self.whole[...] = total.astype(jnp.bfloat16)
+        own = self.stretch(self.my_lon)
+        self.result[own, :] = self.whole[...]
+        for step in range(1, self.lon):
+            peer = lax.rem(self.my_lon + step, self.lon)
+            slot = self.lon + self.lat - 2 + step
+            self.send(self.whole, self.result.at[own], slot, {"lon": peer})
+
+    def finish(self):
+        self.settle()
+
+
+def greet(sizes):
+    lon, lat = sizes
+    barrier = pltpu.get_barrier_semaphore()
+    my_lon, my_lat, my_ch = (lax.axis_index(name) for name in ("lon", "lat", "ch"))
+    pl.semaphore_signal(barrier, inc=1, device_id={"ch": 1 - my_ch}, device_id_type=MESH)
+    for step in range(1, lon):
+        peer = lax.rem(my_lon + step, lon)
+        pl.semaphore_signal(barrier, inc=1, device_id={"lon": peer}, device_id_type=MESH)
+    for step in range(1, lat):
+        peer = lax.rem(my_lat + step, lat)
+        pl.semaphore_signal(barrier, inc=1, device_id={"lat": peer}, device_id_type=MESH)
+    pl.semaphore_wait(barrier, lon + lat - 1)
+
+
+def sum_kernel(sizes, count, *refs):
+    sources, results, rest = refs[:count], refs[count : 2 * count], refs[2 * count :]
+    greet(sizes)
+    sums = []
+    for index in range(count):
+        mine = rest[8 * index : 8 * index + 8]
+        sums.append(GradSum(sizes, sources[index], results[index], mine[:6], mine[6:]))
+    stages = ("start_ch", "start_lon", "start_lat", "start_gather", "finish")
+    for tick in range(count + len(stages) - 1):
+        for index in range(count):
+            if 0 <= tick - index < len(stages):
+                getattr(sums[index], stages[tick - index])()
+
+
+def summed_grads(terms, sizes):
+    width = terms[0].shape[1] // 2
+    scratch = []
+    for term in terms:
+        scratch += GradSum.scratch(sizes, term.shape[0], width)
+    vmem = pl.BlockSpec(memory_space=pltpu.VMEM)
+    return pl.pallas_call(
+        functools.partial(sum_kernel, sizes, len(terms)),
+        out_shape=[jax.ShapeDtypeStruct((t.shape[0], width), jnp.bfloat16) for t in terms],
+        in_specs=[vmem] * len(terms),
+        out_specs=[vmem] * len(terms),
+        scratch_shapes=scratch,
+        compiler_params=pltpu.CompilerParams(
+            collective_id=0, has_side_effects=True, vmem_limit_bytes=48 << 20
+        ),
+    )(*terms)
 
 
 def passed_along(value, axis, steps):
@@ -187,17 +331,11 @@
         (((0,), (0,)), ((), ())),
         preferred_element_type=jnp.float32,
     )
-    block_stack = jnp.concatenate(weight_terms, axis=0)
     own_width = channels // lax.axis_size("ch")
-    block_part, encoder_part = (
-        lax.psum_scatter(
-            block_stack.astype(jnp.bfloat16), "ch", scatter_dimension=1, tiled=True
-        ).astype(jnp.float32),
-        lax.psum_scatter(
-            encoder_term.astype(jnp.bfloat16), "ch", scatter_dimension=1, tiled=True
-        ).astype(jnp.float32),
-    )
-    block_sum, encoder_sum = lax.psum((block_part, encoder_part), ("lon", "lat"))
+    sizes = (lax.axis_size("lon"), lax.axis_size("lat"))
+    terms = [term.astype(jnp.bfloat16) for term in weight_terms[::-1] + [encoder_term]]
+    sums = [value.astype(jnp.float32) for value in summed_grads(terms, sizes)]
+    block_sum, encoder_sum = jnp.stack(sums[:-1][::-1]), sums[-1]
     cells_total = cell_count * lax.axis_size("lon") * lax.axis_size(("lat", "ch"))
     normalizer = 1.0 / math.sqrt(cells_total)
     block_grads = (block_sum * normalizer).reshape(layers, basis_count * channels, own_width)

time: 205 us -> 132 us (0.64)
  blocking collectives: 74.7 us -> 0 us
  Pallas kernels: 0 us -> 41.4 us
  waiting for transfers between devices: 39.8 us -> 20.4 us
  between operations: 14.7 us -> 1.31 us
  local copies, waits for them, and re-layouts: 15.9 us -> 9.76 us
    psum x1 -> x0, blocking collectives: 74.7 us -> none  [per_device(): lax.psum((block_part, encoder_part), ('lon', 'lat'))]
    pallas_call x0 -> x1, Pallas kernels: none -> 41.4 us  [summed_grads(): pl.pallas_call(functools.partial(sum_kernel, sizes, len(terms)), out_shap...]
    unnamed x4 -> x0, waiting for transfers between devices: 17.9 us -> none
    unnamed x28 -> x22, local copies, waits for them, and re-layouts: 7.76 us -> 1.58 us
  transfers between devices with their start and end apart: 22 -> 20, of which waited for: 12 -> 10; matrix products, arithmetic and copies ran while one was open for 5% -> 5% of each run, Pallas kernels for 0% -> 0%
where the time goes in v1:
time: 132 us
  starting transfers between devices  42.5 us (32%)
  Pallas kernels  41.4 us (31%)
  waiting for transfers between devices  20.4 us (15%)
  local copies, waits for them, and re-layouts  9.76 us (7%)
  matrix products  8.68 us (7%)
  other arithmetic  7.51 us (6%)
    pallas_call x1, Pallas kernels, summed_grads(): pl.pallas_call(functools.partial(sum_kernel, sizes, len(terms)), out_shap...  41.4 us
    ppermute x5, starting transfers between devices, padded(): lax.ppermute(lax.slice_in_dim(block, 0, width, axis=dim), axis, backward)  12.4 us
    ppermute x6, starting transfers between devices, from_behind(): return lax.ppermute(block, axis, route)  11.3 us
    ppermute x5, starting transfers between devices, padded(): lax.ppermute(lax.slice_in_dim(block, block.shape[dim] - width, None, axis...  11 us
    ppermute x4, starting transfers between devices, passed_along(): return lax.ppermute(value, axis, pairs)  7.88 us
    ppermute x6, waiting for transfers between devices, from_behind(): return lax.ppermute(block, axis, route)  6.47 us
    ppermute x4, waiting for transfers between devices, passed_along(): return lax.ppermute(value, axis, pairs)  6.05 us
    ppermute x5, waiting for transfers between devices, padded(): lax.ppermute(lax.slice_in_dim(block, block.shape[dim] - width, None, axis...  4.66 us
  transfers between devices with their start and end apart: 20, of which 10 were waited for; matrix products, arithmetic and copies ran while one was open for 5% of the time, Pallas kernels for 0%

profile of v1, /device:TPU:0, one launch (start us, length us, event | category | flops | bytes accessed | tf_op | source)
XLA Modules:
  0.0 131.5 jit_solution(15159985610136835188)
XLA Ops:
  0.7 1.0 fusion.64
  1.6 3.1 %collective-permute-start = (bf16[32,2,128]{2,1,0:T(2,128)(2,1)S(1)}, bf16[32,2,128]{2,1,0:T(2,128)(2,1)S(1)}, u32[]{:S(2)}, u32[]{:S(2)}) collective-permute-start(bf16[32,2,128]{2,1,0:T(2,128)(2,1)S(1)} %get-tuple-element.29), channel_id=1, source_target_pairs={{0,4},{4,8},{8,12},{12,0},{1,5},{5,9},{9,13},{13,1},{2,6},{6,10},{... | collective-permute-start | bytes 49160 | tf_op jit(solution)/shard_map/ppermute | solution.py:175
  4.7 2.1 %collective-permute-start.1 = (bf16[32,2,128]{2,1,0:T(2,128)(2,1)S(1)}, bf16[32,2,128]{2,1,0:T(2,128)(2,1)S(1)}, u32[]{:S(2)}, u32[]{:S(2)}) collective-permute-start(bf16[32,2,128]{2,1,0:T(2,128)(2,1)S(1)} %get-tuple-element.30), channel_id=1, source_target_pairs={{4,0},{8,4},{12,8},{0,12},{5,1},{9,5},{13,9},{1,13},{6,2},{10,6},{... | collective-permute-start | bytes 49160 | tf_op jit(solution)/shard_map/ppermute | solution.py:178
  6.8 0.7 convert_element_type.150
  7.5 0.7 broadcast_compare_fusion
  8.2 0.8 select_bitcast_fusion
  9.1 0.7 subtract_add_fusion
  9.7 1.8 %slice.167 = bf16[32,16,128]{2,1,0:T(8,128)(2,1)S(1)} slice(bf16[32,32,128]{2,1,0:T(8,128)(2,1)} %param.8), slice={[0:32:1], [0:32:2], [0:128:1]} | slice | bytes 262144 | tf_op jit(solution)/shard_map/slice | solution.py:253
  12.2 0.5 slice.171
  12.8 0.5 slice.169
  13.3 0.4 slice.165
  14.2 1.0 add_convert_fusion
  16.0 1.5 %collective-permute-start.2 = (bf16[1,8192]{1,0:T(2,128)(2,1)S(1)}, bf16[1,8192]{1,0:T(2,128)(2,1)S(1)}, u32[]{:S(2)}, u32[]{:S(2)}) collective-permute-start(bf16[1,8192]{1,0:T(2,128)(2,1)S(1)} %get-tuple-element.17), channel_id=1, source_target_pairs={{0,1},{1,2},{2,3},{4,5},{5,6},{6,7},{8,9},{9,10},{10,11},{12,13},{... | collective-permute-start | bytes 49160 | tf_op jit(solution)/shard_map/ppermute | solution.py:165
  17.4 1.3 collective-permute-start.3
  18.7 3.5 %collective-permute-done.3 = bf16[1,8192]{1,0:T(2,128)(2,1)S(1)} collective-permute-done((bf16[1,8192]{1,0:T(2,128)(2,1)S(1)}, bf16[1,8192]{1,0:T(2,128)(2,1)S(1)}, u32[]{:S(2)}, u32[]{:S(2)}) %collective-permute-start.3) | collective-permute-done | bytes 16416 | tf_op jit(solution)/shard_map/ppermute | solution.py:165
  22.8 4.5 %collective-permute-start.4 = (bf16[1,16,256]{2,1,0:T(8,128)(2,1)S(1)}, bf16[1,16,256]{2,1,0:T(8,128)(2,1)S(1)}, u32[]{:S(2)}, u32[]{:S(2)}) collective-permute-start(bf16[1,16,256]{2,1,0:T(8,128)(2,1)S(1)} %get-tuple-element.37), channel_id=1, source_target_pairs={{0,1},{1,2},{2,3},{4,5},{5,6},{6,7},{8,9},{9,10},{10,11},{12,13},{... | collective-permute-start | bytes 24584 | tf_op jit(solution)/shard_map/ppermute | solution.py:175
  27.3 1.3 collective-permute-start.5
  29.0 1.4 %collective-permute-done.5 = bf16[1,16,256]{2,1,0:T(8,128)(2,1)S(1)} collective-permute-done((bf16[1,16,256]{2,1,0:T(8,128)(2,1)S(1)}, bf16[1,16,256]{2,1,0:T(8,128)(2,1)S(1)}, u32[]{:S(2)}, u32[]{:S(2)}) %collective-permute-start.5) | collective-permute-done | bytes 8224 | tf_op jit(solution)/shard_map/ppermute | solution.py:178
  30.5 3.8 %collective-permute-start.7 = (bf16[18,8,256]{2,1,0:T(8,128)(2,1)S(1)}, bf16[18,8,256]{2,1,0:T(8,128)(2,1)S(1)}, u32[]{:S(2)}, u32[]{:S(2)}) collective-permute-start(bf16[18,8,256]{2,1,0:T(8,128)(2,1)S(1)} %get-tuple-element.34), channel_id=1, source_target_pairs={{4,0},{8,4},{12,8},{0,12},{5,1},{9,5},{13,9},{1,13},{6,2},{10,6},{... | collective-permute-start | bytes 221192 | tf_op jit(solution)/shard_map/ppermute | solution.py:178
  34.4 2.3 %collective-permute-done.6 = bf16[18,8,256]{2,1,0:T(8,128)(2,1)S(1)} collective-permute-done((bf16[18,8,256]{2,1,0:T(8,128)(2,1)S(1)}, bf16[18,8,256]{2,1,0:T(8,128)(2,1)S(1)}, u32[]{:S(2)}, u32[]{:S(2)}) %collective-permute-start.6) | collective-permute-done | bytes 73760 | tf_op jit(solution)/shard_map/ppermute | solution.py:175
  38.0 0.8 copy-done.3
  38.8 1.0 fusion.37
  39.9 3.2 %collective-permute-start.8 = (bf16[1,16,256]{2,1,0:T(8,128)(2,1)S(1)}, bf16[1,16,256]{2,1,0:T(8,128)(2,1)S(1)}, u32[]{:S(2)}, u32[]{:S(2)}) collective-permute-start(bf16[1,16,256]{2,1,0:T(8,128)(2,1)S(1)} %get-tuple-element.35), channel_id=1, source_target_pairs={{0,1},{1,2},{2,3},{4,5},{5,6},{6,7},{8,9},{9,10},{10,11},{12,13},{... | collective-permute-start | bytes 24584 | tf_op jit(solution)/shard_map/ppermute | solution.py:175
  43.1 1.3 collective-permute-start.9
  44.4 1.8 %collective-permute-done.9 = bf16[1,16,256]{2,1,0:T(8,128)(2,1)S(1)} collective-permute-done((bf16[1,16,256]{2,1,0:T(8,128)(2,1)S(1)}, bf16[1,16,256]{2,1,0:T(8,128)(2,1)S(1)}, u32[]{:S(2)}, u32[]{:S(2)}) %collective-permute-start.9) | collective-permute-done | bytes 8224 | tf_op jit(solution)/shard_map/ppermute | solution.py:178
  46.4 3.9 %collective-permute-start.11 = (bf16[18,8,256]{2,1,0:T(8,128)(2,1)S(1)}, bf16[18,8,256]{2,1,0:T(8,128)(2,1)S(1)}, u32[]{:S(2)}, u32[]{:S(2)}) collective-permute-start(bf16[18,8,256]{2,1,0:T(8,128)(2,1)S(1)} %get-tuple-element.32), channel_id=1, source_target_pairs={{4,0},{8,4},{12,8},{0,12},{5,1},{9,5},{13,9},{1,13},{6,2},{10,6},{... | collective-permute-start | bytes 221192 | tf_op jit(solution)/shard_map/ppermute | solution.py:178
  50.2 2.4 %collective-permute-done.10 = bf16[18,8,256]{2,1,0:T(8,128)(2,1)S(1)} collective-permute-done((bf16[18,8,256]{2,1,0:T(8,128)(2,1)S(1)}, bf16[18,8,256]{2,1,0:T(8,128)(2,1)S(1)}, u32[]{:S(2)}, u32[]{:S(2)}) %collective-permute-start.10) | collective-permute-done | bytes 73760 | tf_op jit(solution)/shard_map/ppermute | solution.py:175
  53.9 0.5 copy-done.9
  54.4 1.1 fusion.35
  57.2 1.3 collective-permute-start.12
  58.5 2.7 %collective-permute-start.13 = (bf16[18,8,256]{2,1,0:T(8,128)(2,1)S(1)}, bf16[18,8,256]{2,1,0:T(8,128)(2,1)S(1)}, u32[]{:S(2)}, u32[]{:S(2)}) collective-permute-start(bf16[18,8,256]{2,1,0:T(8,128)(2,1)S(1)} %get-tuple-element.26), channel_id=1, source_target_pairs={{0,12},{4,0},{8,4},{12,8},{1,13},{5,1},{9,5},{13,9},{2,14},{6,2},{... | collective-permute-start | bytes 221192 | tf_op jit(solution)/shard_map/ppermute | solution.py:159
  61.2 2.4 %collective-permute-done.12 = bf16[18,8,256]{2,1,0:T(8,128)(2,1)S(1)} collective-permute-done((bf16[18,8,256]{2,1,0:T(8,128)(2,1)S(1)}, bf16[18,8,256]{2,1,0:T(8,128)(2,1)S(1)}, u32[]{:S(2)}, u32[]{:S(2)}) %collective-permute-start.12) | collective-permute-done | bytes 73760 | tf_op jit(solution)/shard_map/ppermute | solution.py:159
  63.6 1.9 %collective-permute-done.13 = bf16[18,8,256]{2,1,0:T(8,128)(2,1)S(1)} collective-permute-done((bf16[18,8,256]{2,1,0:T(8,128)(2,1)S(1)}, bf16[18,8,256]{2,1,0:T(8,128)(2,1)S(1)}, u32[]{:S(2)}, u32[]{:S(2)}) %collective-permute-start.13) | collective-permute-done | bytes 73760 | tf_op jit(solution)/shard_map/ppermute | solution.py:159
  65.6 2.1 %collective-permute-start.14 = (f32[1,16,256]{2,1,0:T(8,128)S(1)}, f32[1,16,256]{2,1,0:T(8,128)S(1)}, u32[]{:S(2)}, u32[]{:S(2)}) collective-permute-start(f32[1,16,256]{2,1,0:T(8,128)S(1)} %get-tuple-element.23), channel_id=1, source_target_pairs={{0,1},{1,2},{2,3},{4,5},{5,6},{6,7},{8,9},{9,10},{10,11},{12,13},{... | collective-permute-start | bytes 49160 | tf_op jit(solution)/shard_map/ppermute | solution.py:165
  67.7 1.4 %collective-permute-start.15 = (f32[1,16,256]{2,1,0:T(8,128)S(1)}, f32[1,16,256]{2,1,0:T(8,128)S(1)}, u32[]{:S(2)}, u32[]{:S(2)}) collective-permute-start(f32[1,16,256]{2,1,0:T(8,128)S(1)} %get-tuple-element.24), channel_id=1, source_target_pairs={{1,0},{2,1},{3,2},{5,4},{6,5},{7,6},{9,8},{10,9},{11,10},{13,12},{... | collective-permute-start | bytes 49160 | tf_op jit(solution)/shard_map/ppermute | solution.py:165
  69.5 1.4 %collective-permute-done.15 = f32[1,16,256]{2,1,0:T(8,128)S(1)} collective-permute-done((f32[1,16,256]{2,1,0:T(8,128)S(1)}, f32[1,16,256]{2,1,0:T(8,128)S(1)}, u32[]{:S(2)}, u32[]{:S(2)}) %collective-permute-start.15) | collective-permute-done | bytes 16416 | tf_op jit(solution)/shard_map/ppermute | solution.py:165
  71.1 1.1 convolution_convert_fusion.3
  72.2 1.4 %reshape.125 = bf16[16,16,4,256]{3,2,1,0:T(4,128)(2,1)S(1)} reshape(bf16[256,1024]{1,0:T(8,128)(2,1)} %convolution_convert_fusion.3) | data formatting | bytes 1048576 | tf_op jit(solution)/shard_map/reshape | solution.py:324
  74.7 1.1 collective-permute-start.16
  75.8 2.8 %collective-permute-start.17 = (bf16[18,8,256]{2,1,0:T(8,128)(2,1)S(1)}, bf16[18,8,256]{2,1,0:T(8,128)(2,1)S(1)}, u32[]{:S(2)}, u32[]{:S(2)}) collective-permute-start(bf16[18,8,256]{2,1,0:T(8,128)(2,1)S(1)} %get-tuple-element.22), channel_id=1, source_target_pairs={{0,12},{4,0},{8,4},{12,8},{1,13},{5,1},{9,5},{13,9},{2,14},{6,2},{... | collective-permute-start | bytes 221192 | tf_op jit(solution)/shard_map/ppermute | solution.py:159
  78.6 0.7 add_convert_fusion.1
  79.3 1.7 %collective-permute-done.16 = bf16[18,8,256]{2,1,0:T(8,128)(2,1)S(1)} collective-permute-done((bf16[18,8,256]{2,1,0:T(8,128)(2,1)S(1)}, bf16[18,8,256]{2,1,0:T(8,128)(2,1)S(1)}, u32[]{:S(2)}, u32[]{:S(2)}) %collective-permute-start.16) | collective-permute-done | bytes 73760 | tf_op jit(solution)/shard_map/ppermute | solution.py:159
  81.1 3.8 %collective-permute-start.18 = (f32[1,16,256]{2,1,0:T(8,128)S(1)}, f32[1,16,256]{2,1,0:T(8,128)S(1)}, u32[]{:S(2)}, u32[]{:S(2)}) collective-permute-start(f32[1,16,256]{2,1,0:T(8,128)S(1)} %get-tuple-element.19), channel_id=1, source_target_pairs={{0,1},{1,2},{2,3},{4,5},{5,6},{6,7},{8,9},{9,10},{10,11},{12,13},{... | collective-permute-start | bytes 49160 | tf_op jit(solution)/shard_map/ppermute | solution.py:165
  84.8 1.3 collective-permute-start.19
  86.5 1.5 %collective-permute-done.19 = f32[1,16,256]{2,1,0:T(8,128)S(1)} collective-permute-done((f32[1,16,256]{2,1,0:T(8,128)S(1)}, f32[1,16,256]{2,1,0:T(8,128)S(1)}, u32[]{:S(2)}, u32[]{:S(2)}) %collective-permute-start.19) | collective-permute-done | bytes 16416 | tf_op jit(solution)/shard_map/ppermute | solution.py:165
  88.4 41.4 %shard_map.111 = (bf16[1024,128]{1,0:T(8,128)(2,1)S(1)}, bf16[1024,128]{1,0:T(8,128)(2,1)S(1)}, bf16[512,128]{1,0:T(8,128)(2,1)S(1)}) custom-call(bf16[1024,256]{1,0:T(8,128)(2,1)S(1)} %convolution_convert_fusion.2.refs_0_, bf16[1024,256]{1,0:T(8,128)(2,1)S(1)} %convolution_convert_fusion.1.refs_1_, bf16[512,256]{1,0:T(8,128)(2,1)S(1)} %convolution_convert_fusion.5.refs_2_), custom_call_target="tpu_custom_call" | custom-call | tf_op jit(solution)/shard_map/pallas_call | solution.py:144
  129.7 0.7 convert_multiply_fusion.1
  130.5 1.0 convert_multiply_fusion
  (94 shorter events, 9.5 us)
Async XLA Ops:
  0.6 21.9 %copy-start = (bf16[512,256]{1,0:T(8,128)(2,1)S(1)}, bf16[512,256]{1,0:T(8,128)(2,1)}, u32[]{:S(2)}) copy-start(bf16[512,256]{1,0:T(8,128)(2,1)} %param.11) | copy-start | bytes 786436
  0.6 11.4 %copy-start.5 = (bf16[32,32,128]{2,1,0:T(8,128)(2,1)S(1)}, bf16[32,32,128]{2,1,0:T(8,128)(2,1)}, u32[]{:S(2)}) copy-start(bf16[32,32,128]{2,1,0:T(8,128)(2,1)} %param.8) | copy-start | bytes 786436
  1.6 10.4 %collective-permute-start = (bf16[32,2,128]{2,1,0:T(2,128)(2,1)S(1)}, bf16[32,2,128]{2,1,0:T(2,128)(2,1)S(1)}, u32[]{:S(2)}, u32[]{:S(2)}) collective-permute-start(bf16[32,2,128]{2,1,0:T(2,128)(2,1)S(1)} %get-tuple-element.29), channel_id=1, source_target_pairs={{0,4},{4,8},{8,12},{12,0},{1,5},{5,9},{9,13},{13,1},{2,6},{6,10},{... | collective-permute-start | bytes 49160 | tf_op jit(solution)/shard_map/ppermute | solution.py:175
  4.7 7.3 %collective-permute-start.1 = (bf16[32,2,128]{2,1,0:T(2,128)(2,1)S(1)}, bf16[32,2,128]{2,1,0:T(2,128)(2,1)S(1)}, u32[]{:S(2)}, u32[]{:S(2)}) collective-permute-start(bf16[32,2,128]{2,1,0:T(2,128)(2,1)S(1)} %get-tuple-element.30), channel_id=1, source_target_pairs={{4,0},{8,4},{12,8},{0,12},{5,1},{9,5},{13,9},{1,13},{6,2},{10,6},{... | collective-permute-start | bytes 49160 | tf_op jit(solution)/shard_map/ppermute | solution.py:178
  16.0 2.8 %collective-permute-start.2 = (bf16[1,8192]{1,0:T(2,128)(2,1)S(1)}, bf16[1,8192]{1,0:T(2,128)(2,1)S(1)}, u32[]{:S(2)}, u32[]{:S(2)}) collective-permute-start(bf16[1,8192]{1,0:T(2,128)(2,1)S(1)} %get-tuple-element.17), channel_id=1, source_target_pairs={{0,1},{1,2},{2,3},{4,5},{5,6},{6,7},{8,9},{9,10},{10,11},{12,13},{... | collective-permute-start | bytes 49160 | tf_op jit(solution)/shard_map/ppermute | solution.py:165
  17.4 4.8 %collective-permute-start.3 = (bf16[1,8192]{1,0:T(2,128)(2,1)S(1)}, bf16[1,8192]{1,0:T(2,128)(2,1)S(1)}, u32[]{:S(2)}, u32[]{:S(2)}) collective-permute-start(bf16[1,8192]{1,0:T(2,128)(2,1)S(1)} %get-tuple-element.18), channel_id=1, source_target_pairs={{1,0},{2,1},{3,2},{5,4},{6,5},{7,6},{9,8},{10,9},{11,10},{13,12},{... | collective-permute-start | bytes 49160 | tf_op jit(solution)/shard_map/ppermute | solution.py:165
  22.8 6.2 %collective-permute-start.4 = (bf16[1,16,256]{2,1,0:T(8,128)(2,1)S(1)}, bf16[1,16,256]{2,1,0:T(8,128)(2,1)S(1)}, u32[]{:S(2)}, u32[]{:S(2)}) collective-permute-start(bf16[1,16,256]{2,1,0:T(8,128)(2,1)S(1)} %get-tuple-element.37), channel_id=1, source_target_pairs={{0,1},{1,2},{2,3},{4,5},{5,6},{6,7},{8,9},{9,10},{10,11},{12,13},{... | collective-permute-start | bytes 24584 | tf_op jit(solution)/shard_map/ppermute | solution.py:175
  27.3 3.1 %collective-permute-start.5 = (bf16[1,16,256]{2,1,0:T(8,128)(2,1)S(1)}, bf16[1,16,256]{2,1,0:T(8,128)(2,1)S(1)}, u32[]{:S(2)}, u32[]{:S(2)}) collective-permute-start(bf16[1,16,256]{2,1,0:T(8,128)(2,1)S(1)} %get-tuple-element.38), channel_id=1, source_target_pairs={{1,0},{2,1},{3,2},{5,4},{6,5},{7,6},{9,8},{10,9},{11,10},{13,12},{... | collective-permute-start | bytes 24584 | tf_op jit(solution)/shard_map/ppermute | solution.py:178
  30.4 6.3 %collective-permute-start.6 = (bf16[18,8,256]{2,1,0:T(8,128)(2,1)S(1)}, bf16[18,8,256]{2,1,0:T(8,128)(2,1)S(1)}, u32[]{:S(2)}, u32[]{:S(2)}) collective-permute-start(bf16[18,8,256]{2,1,0:T(8,128)(2,1)S(1)} %get-tuple-element.33), channel_id=1, source_target_pairs={{0,4},{4,8},{8,12},{12,0},{1,5},{5,9},{9,13},{13,1},{2,6},{6,10},{... | collective-permute-start | bytes 221192 | tf_op jit(solution)/shard_map/ppermute | solution.py:175
  30.5 6.2 %collective-permute-start.7 = (bf16[18,8,256]{2,1,0:T(8,128)(2,1)S(1)}, bf16[18,8,256]{2,1,0:T(8,128)(2,1)S(1)}, u32[]{:S(2)}, u32[]{:S(2)}) collective-permute-start(bf16[18,8,256]{2,1,0:T(8,128)(2,1)S(1)} %get-tuple-element.34), channel_id=1, source_target_pairs={{4,0},{8,4},{12,8},{0,12},{5,1},{9,5},{13,9},{1,13},{6,2},{10,6},{... | collective-permute-start | bytes 221192 | tf_op jit(solution)/shard_map/ppermute | solution.py:178
  37.6 1.2 copy-start.3
  39.9 4.5 %collective-permute-start.8 = (bf16[1,16,256]{2,1,0:T(8,128)(2,1)S(1)}, bf16[1,16,256]{2,1,0:T(8,128)(2,1)S(1)}, u32[]{:S(2)}, u32[]{:S(2)}) collective-permute-start(bf16[1,16,256]{2,1,0:T(8,128)(2,1)S(1)} %get-tuple-element.35), channel_id=1, source_target_pairs={{0,1},{1,2},{2,3},{4,5},{5,6},{6,7},{8,9},{9,10},{10,11},{12,13},{... | collective-permute-start | bytes 24584 | tf_op jit(solution)/shard_map/ppermute | solution.py:175
  43.1 3.1 %collective-permute-start.9 = (bf16[1,16,256]{2,1,0:T(8,128)(2,1)S(1)}, bf16[1,16,256]{2,1,0:T(8,128)(2,1)S(1)}, u32[]{:S(2)}, u32[]{:S(2)}) collective-permute-start(bf16[1,16,256]{2,1,0:T(8,128)(2,1)S(1)} %get-tuple-element.36), channel_id=1, source_target_pairs={{1,0},{2,1},{3,2},{5,4},{6,5},{7,6},{9,8},{10,9},{11,10},{13,12},{... | collective-permute-start | bytes 24584 | tf_op jit(solution)/shard_map/ppermute | solution.py:178
  46.3 6.3 %collective-permute-start.10 = (bf16[18,8,256]{2,1,0:T(8,128)(2,1)S(1)}, bf16[18,8,256]{2,1,0:T(8,128)(2,1)S(1)}, u32[]{:S(2)}, u32[]{:S(2)}) collective-permute-start(bf16[18,8,256]{2,1,0:T(8,128)(2,1)S(1)} %get-tuple-element.31), channel_id=1, source_target_pairs={{0,4},{4,8},{8,12},{12,0},{1,5},{5,9},{9,13},{13,1},{2,6},{6,10},{... | collective-permute-start | bytes 221192 | tf_op jit(solution)/shard_map/ppermute | solution.py:175
  46.4 6.2 %collective-permute-start.11 = (bf16[18,8,256]{2,1,0:T(8,128)(2,1)S(1)}, bf16[18,8,256]{2,1,0:T(8,128)(2,1)S(1)}, u32[]{:S(2)}, u32[]{:S(2)}) collective-permute-start(bf16[18,8,256]{2,1,0:T(8,128)(2,1)S(1)} %get-tuple-element.32), channel_id=1, source_target_pairs={{4,0},{8,4},{12,8},{0,12},{5,1},{9,5},{13,9},{1,13},{6,2},{10,6},{... | collective-permute-start | bytes 221192 | tf_op jit(solution)/shard_map/ppermute | solution.py:178
  53.5 0.9 copy-start.9
  53.9 1.6 %copy-start.1 = (bf16[32,8,4,256]{3,1,2,0:T(8,128)(2,1)}, bf16[32,8,4,256]{3,1,2,0:T(8,128)(2,1)S(1)}, u32[]{:S(2)}) copy-start(bf16[32,8,4,256]{3,1,2,0:T(8,128)(2,1)S(1)} %copy.79) | copy-start | bytes 1572868
  57.2 11.9 %copy-start.2 = (bf16[32,8,4,256]{3,1,2,0:T(8,128)(2,1)S(1)}, bf16[32,8,4,256]{3,1,2,0:T(8,128)(2,1)}, u32[]{:S(2)}) copy-start(bf16[32,8,4,256]{3,1,2,0:T(8,128)(2,1)} %copy-done.1) | copy-start | bytes 1572868
  57.2 6.4 %collective-permute-start.12 = (bf16[18,8,256]{2,1,0:T(8,128)(2,1)S(1)}, bf16[18,8,256]{2,1,0:T(8,128)(2,1)S(1)}, u32[]{:S(2)}, u32[]{:S(2)}) collective-permute-start(bf16[18,8,256]{2,1,0:T(8,128)(2,1)S(1)} %get-tuple-element.25), channel_id=1, source_target_pairs={{0,4},{4,8},{8,12},{12,0},{1,5},{5,9},{9,13},{13,1},{2,6},{6,10},{... | collective-permute-start | bytes 221192 | tf_op jit(solution)/shard_map/ppermute | solution.py:159
  58.5 7.0 %collective-permute-start.13 = (bf16[18,8,256]{2,1,0:T(8,128)(2,1)S(1)}, bf16[18,8,256]{2,1,0:T(8,128)(2,1)S(1)}, u32[]{:S(2)}, u32[]{:S(2)}) collective-permute-start(bf16[18,8,256]{2,1,0:T(8,128)(2,1)S(1)} %get-tuple-element.26), channel_id=1, source_target_pairs={{0,12},{4,0},{8,4},{12,8},{1,13},{5,1},{9,5},{13,9},{2,14},{6,2},{... | collective-permute-start | bytes 221192 | tf_op jit(solution)/shard_map/ppermute | solution.py:159
  65.6 5.4 %copy-start.7 = (f32[256,256]{1,0:T(8,128)S(1)}, f32[256,256]{1,0:T(8,128)}, u32[]{:S(2)}) copy-start(f32[256,256]{1,0:T(8,128)} %get-tuple-element.47) | copy-start | bytes 786436
  65.6 3.9 %collective-permute-start.14 = (f32[1,16,256]{2,1,0:T(8,128)S(1)}, f32[1,16,256]{2,1,0:T(8,128)S(1)}, u32[]{:S(2)}, u32[]{:S(2)}) collective-permute-start(f32[1,16,256]{2,1,0:T(8,128)S(1)} %get-tuple-element.23), channel_id=1, source_target_pairs={{0,1},{1,2},{2,3},{4,5},{5,6},{6,7},{8,9},{9,10},{10,11},{12,13},{... | collective-permute-start | bytes 49160 | tf_op jit(solution)/shard_map/ppermute | solution.py:165
  67.7 3.4 %copy-start.4 = (bf16[2,1024,256]{2,1,0:T(8,128)(2,1)S(1)}, bf16[2,1024,256]{2,1,0:T(8,128)(2,1)}, u32[]{:S(2)}) copy-start(bf16[2,1024,256]{2,1,0:T(8,128)(2,1)} %param.14) | copy-start | bytes 3145732
  67.7 3.3 %collective-permute-start.15 = (f32[1,16,256]{2,1,0:T(8,128)S(1)}, f32[1,16,256]{2,1,0:T(8,128)S(1)}, u32[]{:S(2)}, u32[]{:S(2)}) collective-permute-start(f32[1,16,256]{2,1,0:T(8,128)S(1)} %get-tuple-element.24), channel_id=1, source_target_pairs={{1,0},{2,1},{3,2},{5,4},{6,5},{7,6},{9,8},{10,9},{11,10},{13,12},{... | collective-permute-start | bytes 49160 | tf_op jit(solution)/shard_map/ppermute | solution.py:165
  74.5 4.1 %copy-start.8 = (f32[256,256]{1,0:T(8,128)S(1)}, f32[256,256]{1,0:T(8,128)}, u32[]{:S(2)}) copy-start(f32[256,256]{1,0:T(8,128)} %get-tuple-element.28) | copy-start | bytes 786436
  74.7 6.3 %collective-permute-start.16 = (bf16[18,8,256]{2,1,0:T(8,128)(2,1)S(1)}, bf16[18,8,256]{2,1,0:T(8,128)(2,1)S(1)}, u32[]{:S(2)}, u32[]{:S(2)}) collective-permute-start(bf16[18,8,256]{2,1,0:T(8,128)(2,1)S(1)} %get-tuple-element.21), channel_id=1, source_target_pairs={{0,4},{4,8},{8,12},{12,0},{1,5},{5,9},{9,13},{13,1},{2,6},{6,10},{... | collective-permute-start | bytes 221192 | tf_op jit(solution)/shard_map/ppermute | solution.py:159
  75.8 5.2 %collective-permute-start.17 = (bf16[18,8,256]{2,1,0:T(8,128)(2,1)S(1)}, bf16[18,8,256]{2,1,0:T(8,128)(2,1)S(1)}, u32[]{:S(2)}, u32[]{:S(2)}) collective-permute-start(bf16[18,8,256]{2,1,0:T(8,128)(2,1)S(1)} %get-tuple-element.22), channel_id=1, source_target_pairs={{0,12},{4,0},{8,4},{12,8},{1,13},{5,1},{9,5},{13,9},{2,14},{6,2},{... | collective-permute-start | bytes 221192 | tf_op jit(solution)/shard_map/ppermute | solution.py:159
  81.1 5.4 %collective-permute-start.18 = (f32[1,16,256]{2,1,0:T(8,128)S(1)}, f32[1,16,256]{2,1,0:T(8,128)S(1)}, u32[]{:S(2)}, u32[]{:S(2)}) collective-permute-start(f32[1,16,256]{2,1,0:T(8,128)S(1)} %get-tuple-element.19), channel_id=1, source_target_pairs={{0,1},{1,2},{2,3},{4,5},{5,6},{6,7},{8,9},{9,10},{10,11},{12,13},{... | collective-permute-start | bytes 49160 | tf_op jit(solution)/shard_map/ppermute | solution.py:165
  84.8 3.2 %collective-permute-start.19 = (f32[1,16,256]{2,1,0:T(8,128)S(1)}, f32[1,16,256]{2,1,0:T(8,128)S(1)}, u32[]{:S(2)}, u32[]{:S(2)}) collective-permute-start(f32[1,16,256]{2,1,0:T(8,128)S(1)} %get-tuple-element.20), channel_id=1, source_target_pairs={{1,0},{2,1},{3,2},{5,4},{6,5},{7,6},{9,8},{10,9},{11,10},{13,12},{... | collective-permute-start | bytes 49160 | tf_op jit(solution)/shard_map/ppermute | solution.py:165
  88.1 42.4 %copy-start.6 = (bf16[16,16,256]{2,1,0:T(8,128)(2,1)}, bf16[16,16,256]{2,1,0:T(8,128)(2,1)S(1)}, u32[]{:S(2)}) copy-start(bf16[16,16,256]{2,1,0:T(8,128)(2,1)S(1)} %fusion.26) | copy-start | bytes 393220

commit v2 on v0

v2 whole, which is shorter than its diff:
```python
import functools
import math

import jax
import jax.numpy as jnp
from jax import lax
from jax.experimental import pallas as pl
from jax.experimental.pallas import tpu as pltpu
from jax.sharding import PartitionSpec as P

REACH = 8
TAP_REACH = 2
TILE = 16
MESH = pl.DeviceIdType.MESH
BF16 = jnp.bfloat16
F32 = jnp.float32


def along(axis, steps):
    count = lax.axis_size(axis)
    return {axis: lax.rem(lax.axis_index(axis) + steps + count, count)}


def neighbour(row_step, col_step):
    ch_count = lax.axis_size("ch")
    bands = lax.axis_size("lat") * ch_count
    band = lax.axis_index("lat") * ch_count + lax.axis_index("ch")
    band = lax.rem(band + row_step + bands, bands)
    target = {}
    if row_step:
        target = {"lat": band // ch_count, "ch": lax.rem(band, ch_count)}
    if col_step:
        target.update(along("lon", col_step))
    return target


AROUND = [(r, c) for r in (-1, 0, 1) for c in (-1, 0, 1) if r or c]


def greet():
    targets = [neighbour(r, c) for r, c in AROUND]
    for axis in ("ch", "lat", "lon"):
        targets += [along(axis, step) for step in range(1, lax.axis_size(axis))]
    barrier = pltpu.get_barrier_semaphore()
    for target in targets:
        pl.semaphore_signal(barrier, inc=1, device_id=target, device_id_type=MESH)
    pl.semaphore_wait(barrier, len(targets))


class Sender:
    def __init__(self, sems):
        self.ssem, self.rsem = sems
        self.pending = []

    def send(self, source, target, slot, device):
        copy = pltpu.make_async_remote_copy(
            src_ref=source,
            dst_ref=target,
            send_sem=self.ssem.at[slot],
            recv_sem=self.rsem.at[slot],
            device_id=device,
            device_id_type=MESH,
        )
        copy.start()
        self.pending.append(copy)

    def settle(self):
        for copy in self.pending:
            copy.wait()
        self.pending = []


class GradSum(Sender):
    def __init__(self, result, bufs):
        super().__init__(bufs[-2:])
        self.result = result
        self.source, self.rec_ch, self.part, self.rec_lat, self.strip, self.rec_lon, self.piece = bufs[:-2]
        self.width = self.part.shape[1]
        self.lat, self.lon = lax.axis_size("lat"), lax.axis_size("lon")
        self.height = self.strip.shape[0]
        self.span = self.piece.shape[0]
        self.split = self.span < self.height

    @staticmethod
    def scratch(sizes, rows, columns):
        lat, lon = sizes
        width = columns // 2
        height = rows // lat
        span = height // lon if height % (lon * TILE) == 0 else height
        count = 1 + 2 * (lat - 1) + 2 * (lon - 1)
        return [
            pltpu.VMEM((rows, columns), BF16),
            pltpu.VMEM((rows, width), BF16),
            pltpu.VMEM((rows, width), BF16),
            pltpu.VMEM((lat - 1, height, width), BF16),
            pltpu.VMEM((height, width), BF16),
            pltpu.VMEM((lon - 1, span, width), BF16),
            pltpu.VMEM((span, width), BF16),
            pltpu.SemaphoreType.DMA((count,)),
            pltpu.SemaphoreType.DMA((count,)),
        ]

    def columns(self, half):
        return pl.ds(pl.multiple_of(half * self.width, self.width), self.width)

    @staticmethod
    def stretch(owner, size):
        return pl.ds(pl.multiple_of(owner * size, size), size)

    def start_ch(self):
        other = 1 - lax.axis_index("ch")
        self.send(self.source.at[:, self.columns(other)], self.rec_ch, 0, {"ch": other})

    def start_lat(self):
        self.settle()
        own = self.source[:, self.columns(lax.axis_index("ch"))].astype(F32)
        self.part[...] = (own + self.rec_ch[...].astype(F32)).astype(BF16)
        for step in range(1, self.lat):
            peer = along("lat", step)
            rows = self.stretch(peer["lat"], self.height)
            self.send(self.part.at[rows], self.rec_lat.at[step - 1], step, peer)

    def start_lon(self):
        self.settle()
        total = self.part[self.stretch(lax.axis_index("lat"), self.height), :].astype(F32)
        for step in range(1, self.lat):
            total = total + self.rec_lat[step - 1].astype(F32)
        self.strip[...] = total.astype(BF16)
        for step in range(1, self.lon):
            peer = along("lon", step)
            source = self.strip
            if self.split:
                source = self.strip.at[self.stretch(peer["lon"], self.span)]
            self.send(source, self.rec_lon.at[step - 1], self.lat + step - 1, peer)

    def gather_lon(self):
        self.settle()
        if self.split:
            total = self.strip[self.stretch(lax.axis_index("lon"), self.span), :].astype(F32)
        else:
            total = self.strip[...].astype(F32)
        for step in range(1, self.lon):
            total = total + self.rec_lon[step - 1].astype(F32)
        self.piece[...] = total.astype(BF16)
        offset = lax.axis_index("lat") * self.height
        if self.split:
            offset = offset + lax.axis_index("lon") * self.span
        rows = pl.ds(pl.multiple_of(offset, TILE), self.span)
        self.result[rows, :] = self.piece[...]
        if self.split:
            for step in range(1, self.lon):
                slot = self.lat + self.lon - 2 + step
                self.send(self.piece, self.result.at[rows], slot, along("lon", step))

    def gather_lat(self):
        self.settle()
        rows = self.stretch(lax.axis_index("lat"), self.height)
        for step in range(1, self.lat):
            slot = self.lat + 2 * self.lon - 3 + step
            self.send(self.result.at[rows], self.result.at[rows], slot, along("lat", step))

    def finish(self):
        self.settle()


STAGES = ("start_ch", "start_lat", "start_lon", "gather_lon", "gather_lat", "finish")


class Halo(Sender):
    def __init__(self, bufs):
        super().__init__(bufs[-2:])
        self.out_side, self.out_row, self.in_side, self.in_row = bufs[:-2]

    @staticmethod
    def scratch(rows, cols, width, row_blocks):
        return [
            pltpu.VMEM((2, rows * REACH, width), BF16),
            pltpu.VMEM((row_blocks, cols, width), BF16),
            pltpu.VMEM((2, rows * REACH, width), BF16),
            pltpu.VMEM((6, cols, width), BF16),
            pltpu.SemaphoreType.DMA((8,)),
            pltpu.SemaphoreType.DMA((8,)),
        ]

    def start(self, row_block_of):
        self.send(self.out_side.at[0], self.in_side.at[1], 0, neighbour(0, -1))
        self.send(self.out_side.at[1], self.in_side.at[0], 1, neighbour(0, 1))
        slot = 2
        for row_step in (-1, 1):
            for col_step in (-1, 0, 1):
                place = (0 if row_step == 1 else 3) + 1 - col_step
                self.send(
                    self.out_row.at[row_block_of(row_step, col_step)],
                    self.in_row.at[place],
                    slot,
                    neighbour(row_step, col_step),
                )
                slot += 1


def edge_flags():
    ch_count = lax.axis_size("ch")
    bands = lax.axis_size("lat") * ch_count
    band = lax.axis_index("lat") * ch_count + lax.axis_index("ch")
    return band > 0, band < bands - 1


def extend(halo, state, ext, rows, cols):
    span = cols + 2 * REACH
    west, east = halo.in_side[0].astype(F32), halo.in_side[1].astype(F32)
    for row in range(rows):
        low, high = row * REACH, (row + 1) * REACH
        line = jnp.concatenate(
            [west[low:high], state[row * cols : (row + 1) * cols], east[low:high]], axis=0
        )
        ext[(row + 1) * span : (row + 2) * span, :] = line.astype(BF16)
    for first, row, flag in zip((0, 3), (0, rows + 1), edge_flags()):
        line = jnp.concatenate(
            [
                halo.in_row[first].astype(F32)[cols - REACH :],
                halo.in_row[first + 1].astype(F32),
                halo.in_row[first + 2].astype(F32)[:REACH],
            ],
            axis=0,
        )
        ext[row * span : (row + 1) * span, :] = jnp.where(flag, line, 0.0).astype(BF16)


def send_state(halo, state, rows, cols):
    pieces = [
        [state[r * cols : r * cols + REACH] for r in range(rows)],
        [state[(r + 1) * cols - REACH : (r + 1) * cols] for r in range(rows)],
    ]
    for side in range(2):
        halo.out_side[side] = jnp.concatenate(pieces[side], axis=0).astype(BF16)
    halo.out_row[0] = state[:cols].astype(BF16)
    halo.out_row[1] = state[(rows - 1) * cols :].astype(BF16)
    halo.start(lambda row_step, col_step: 0 if row_step == -1 else 1)


def send_spread(halo, spread, rows, cols):
    span = cols + 2 * REACH
    west = [spread[(r + 1) * span : (r + 1) * span + REACH, :] for r in range(rows)]
    east = [spread[(r + 2) * span - REACH : (r + 2) * span, :] for r in range(rows)]
    halo.out_side[0] = jnp.concatenate(west, axis=0).astype(BF16)
    halo.out_side[1] = jnp.concatenate(east, axis=0).astype(BF16)
    for block, row in enumerate((0, rows + 1)):
        base = row * span
        halo.out_row[2 * block] = spread[base + REACH : base + REACH + cols, :].astype(BF16)
        corners = [spread[base : base + REACH, :], spread[base + span - REACH : base + span, :]]
        if cols > 2 * REACH:
            corners.insert(1, jnp.zeros((cols - 2 * REACH, spread.shape[1]), F32))
        halo.out_row[2 * block + 1] = jnp.concatenate(corners, axis=0).astype(BF16)
    halo.start(
        lambda row_step, col_step: (0 if row_step == -1 else 2) + (1 if col_step else 0)
    )


def take_spread(halo, spread, gradient, rows, cols):
    span = cols + 2 * REACH
    west, east = halo.in_side[0].astype(F32), halo.in_side[1].astype(F32)
    outer = {}
    for first, row, flag in zip((0, 3), (0, rows - 1), edge_flags()):
        line = halo.in_row[first + 1].astype(F32)
        rim_west = halo.in_row[first].astype(F32)[cols - REACH :]
        rim_east = halo.in_row[first + 2].astype(F32)[:REACH]
        rims = [rim_west, rim_east]
        if cols > 2 * REACH:
            rims.insert(1, jnp.zeros((cols - 2 * REACH, line.shape[1]), F32))
        outer[row] = jnp.where(flag, line + jnp.concatenate(rims, axis=0), 0.0)
    result = []
    for row in range(rows):
        low, high = row * REACH, (row + 1) * REACH
        rims = [west[low:high], east[low:high]]
        if cols > 2 * REACH:
            rims.insert(1, jnp.zeros((cols - 2 * REACH, west.shape[1]), F32))
        base = (row + 1) * span + REACH
        line = spread[base : base + cols, :] + jnp.concatenate(rims, axis=0)
        if row in outer:
            line = line + outer[row]
        result.append(gradient[row * cols : (row + 1) * cols].astype(F32) + line)
    return result


def aligned(index, size):
    return pl.ds(pl.multiple_of(index * size, size), size)


GROUP = 4


def over_rows(rows, body):
    group = GROUP if rows % GROUP == 0 else 1

    def step(index, carry):
        for inner in range(group):
            body(index * group + inner)
        return carry

    lax.fori_loop(0, rows // group, step, 0)


def make_bands(base, bands, rows, cols, basis_count):
    width = base.shape[1]

    def one(row):
        table = base[aligned(row, 2 * basis_count), :]
        for k in range(basis_count):
            line = jnp.broadcast_to(table[k : k + 1], (cols, width))
            moved = pltpu.roll(line, 0, 1, stride=1, stride_axis=0)
            start = pl.multiple_of((row * basis_count + k) * cols, cols)
            bands[pl.ds(start, cols), :] = moved.astype(BF16)

    over_rows(rows, one)


def stencil(bands, ext, features, rows, cols, basis_count):
    span = cols + 2 * REACH
    channels = ext.shape[1]

    def one(row):
        lhs = bands[aligned(row, basis_count * cols), :][:, : 3 * span]
        rhs = ext[pl.ds(pl.multiple_of(row * span, span), 3 * span), :]
        out = jnp.dot(lhs, rhs, preferred_element_type=F32).astype(BF16)
        for k in range(basis_count):
            features[aligned(row, cols), k * channels : (k + 1) * channels] = out[
                k * cols : (k + 1) * cols
            ]

    over_rows(rows, one)


def adjoint(bands, errs, spread, rows, cols, basis_count):
    span = cols + 2 * REACH
    spread[...] = jnp.zeros_like(spread)

    def one(row):
        lhs = bands[aligned(row, basis_count * cols), :][:, : 3 * span]
        rhs = errs[aligned(row, basis_count * cols), :]
        out = lax.dot_general(lhs, rhs, (((0,), (0,)), ((), ())), preferred_element_type=F32)
        place = pl.ds(pl.multiple_of(row * span, span), 3 * span)
        spread[place, :] = spread[place, :] + out

    over_rows(rows, one)


def rows_product(left, right):
    return lax.dot_general(left, right, (((0,), (0,)), ((), ())), preferred_element_type=F32)


def net_kernel(plan, *refs):
    rows, cols, basis_count, layers = plan
    latent_in, encoder_weight, base, weights, cotangent = refs[:5]
    state_out, latent_grad = refs[5:7]
    results = refs[7 : 8 + layers]
    rest = list(refs[8 + layers :])
    bands, ext, spread, errs, features, preact = rest[:6]
    rest = rest[6:]
    halos = []
    for _ in range(2 * layers):
        halos.append(Halo(rest[:6]))
        rest = rest[6:]
    sums = []
    for index in range(layers + 1):
        sums.append(GradSum(results[index], rest[:9]))
        rest = rest[9:]
    channels = ext.shape[1]
    progress = [0] * (layers + 1)

    def advance(index):
        getattr(sums[index], STAGES[progress[index]])()
        progress[index] += 1

    greet()
    state = jnp.dot(latent_in[...], encoder_weight[...], preferred_element_type=F32)
    state = state.astype(BF16).astype(F32)
    for layer in range(layers):
        send_state(halos[layer], state, rows, cols)
        if layer == 0:
            make_bands(base, bands, rows, cols, basis_count)
        halos[layer].settle()
        extend(halos[layer], state, ext, rows, cols)
        stencil(bands, ext, features.at[layer], rows, cols, basis_count)
        pre = jnp.dot(features[layer], weights[layer], preferred_element_type=F32)
        preact[layer] = pre
        state = (state + pre / (1.0 + jnp.exp(-pre))).astype(BF16).astype(F32)
    state_out[...] = state.astype(BF16)

    gradient = cotangent[...].astype(F32)
    for layer in reversed(range(layers)):
        pre = preact[layer]
        sigma = 1.0 / (1.0 + jnp.exp(-pre))
        act_grad = (gradient * sigma * (1.0 + pre * (1.0 - sigma))).astype(BF16)
        for k in range(basis_count):
            block = weights[layer, k * channels : (k + 1) * channels, :]
            out = lax.dot_general(
                act_grad, block, (((1,), (1,)), ((), ())), preferred_element_type=F32
            ).astype(BF16)
            for row in range(rows):
                start = (row * basis_count + k) * cols
                errs[start : start + cols, :] = out[row * cols : (row + 1) * cols]
        adjoint(bands, errs, spread, rows, cols, basis_count)
        halo = halos[layers + layer]
        send_spread(halo, spread, rows, cols)
        sums[layer].source[...] = rows_product(features[layer], act_grad).astype(BF16)
        advance(layer)
        if layer + 1 < layers:
            advance(layer + 1)
        halo.settle()
        lines = take_spread(halo, spread, gradient, rows, cols)
        gradient = jnp.concatenate(lines, axis=0).astype(BF16).astype(F32)
    latent_grad[...] = gradient.astype(BF16)
    sums[layers].source[...] = rows_product(latent_in[...], gradient.astype(BF16)).astype(BF16)
    advance(layers)
    while min(progress) < len(STAGES):
        for index in list(range(layers))[::-1] + [layers]:
            if progress[index] < len(STAGES):
                advance(index)


def run_net(plan, sizes, latent_in, encoder_weight, base, weights, cotangent):
    rows, cols, basis_count, layers = plan
    cells, channels = rows * cols, weights.shape[2]
    features = basis_count * channels
    span = cols + 2 * REACH
    in_features = encoder_weight.shape[0]
    heights = [features] * layers + [in_features]
    scratch = [
        pltpu.VMEM((rows * basis_count * cols, base.shape[1]), BF16),
        pltpu.VMEM(((rows + 2) * span, channels), BF16),
        pltpu.VMEM(((rows + 2) * span, channels), F32),
        pltpu.VMEM((rows * basis_count * cols, channels), BF16),
        pltpu.VMEM((layers, cells, features), BF16),
        pltpu.VMEM((layers, cells, channels), F32),
    ]
    for index in range(2 * layers):
        scratch += Halo.scratch(rows, cols, channels, 2 if index < layers else 4)
    for height in heights:
        scratch += GradSum.scratch(sizes, height, channels)
    vmem = pl.BlockSpec(memory_space=pltpu.VMEM)
    field = jax.ShapeDtypeStruct((cells, channels), BF16)
    grads = [jax.ShapeDtypeStruct((height, channels // 2), BF16) for height in heights]
    return pl.pallas_call(
        functools.partial(net_kernel, plan),
        out_shape=[field, field] + grads,
        in_specs=[vmem] * 5,
        out_specs=[vmem] * (3 + layers),
        scratch_shapes=scratch,
        compiler_params=pltpu.CompilerParams(
            collective_id=0, has_side_effects=True, vmem_limit_bytes=56 << 20
        ),
    )(latent_in, encoder_weight, base, weights, cotangent)


def from_behind(block, axis, distance):
    devices = range(lax.axis_size(axis))
    route = [(i - distance, i) for i in devices if i - distance in devices]
    return lax.ppermute(block, axis, route)


def padded(block, sides, width, periodic):
    for axis, dim in sides:
        count = lax.axis_size(axis)
        forward = [(i, i + 1) for i in range(count - 1)]
        if periodic:
            forward.append((count - 1, 0))
        backward = [(target, source) for source, target in forward]
        low = lax.ppermute(
            lax.slice_in_dim(block, block.shape[dim] - width, None, axis=dim), axis, forward
        )
        high = lax.ppermute(lax.slice_in_dim(block, 0, width, axis=dim), axis, backward)
        block = jnp.concatenate([low, block, high], axis=dim)
    return block


def add_edges(middle, to_first, to_last):
    row_count = middle.shape[0]
    rest_pads = [(0, 0)] * (middle.ndim - 1)
    lower = jnp.pad(to_first, [(0, row_count - 1)] + rest_pads)
    upper = jnp.pad(to_last, [(row_count - 1, 0)] + rest_pads)
    return middle + lower + upper


def per_device(
    input_field,
    encoder_filter,
    row_owner,
    encoder_weight,
    disco_basis,
    row_widths,
    block_weights,
    cotangent,
):
    rows_in, cols_in, in_width = input_field.shape
    rows_dev = rows_in // 2
    cols_dev = cols_in // 2
    basis_count = encoder_filter.shape[1]
    tap_count = encoder_filter.shape[2]
    channels = block_weights.shape[2]
    layers = block_weights.shape[0]
    cell_count = rows_dev * cols_dev
    extended_in = padded(input_field, (("lon", 1),), TAP_REACH, True)
    filter_values = encoder_filter.astype(jnp.float32)
    accumulated = jnp.zeros((rows_in, cols_dev, basis_count, in_width), jnp.float32)
    for tap_index in range(tap_count):
        sampled = extended_in[:, tap_index : tap_index + cols_in : 2, :]
        accumulated = (
            accumulated
            + sampled[:, :, None, :].astype(jnp.float32)
            * filter_values[:, None, :, tap_index, None]
        )
    filtered_in = accumulated.astype(jnp.bfloat16).reshape(
        rows_in, cols_dev * basis_count * in_width
    )
    first_row = lax.axis_index(("lat", "ch")) * rows_dev
    relative = row_owner - first_row + 1
    selector = (relative[None, :] == jnp.arange(rows_dev + 2, dtype=jnp.int32)[:, None]).astype(
        jnp.bfloat16
    )
    summed = jnp.dot(selector, filtered_in, preferred_element_type=jnp.float32)
    from_above = from_behind(summed[0:1].astype(jnp.bfloat16), ("lat", "ch"), -1).astype(
        jnp.float32
    )
    from_below = from_behind(summed[rows_dev + 1 :].astype(jnp.bfloat16), ("lat", "ch"), 1).astype(
        jnp.float32
    )
    regridded = add_edges(summed[1 : rows_dev + 1], from_below, from_above)
    latent_in = regridded.astype(jnp.bfloat16).reshape(cell_count, basis_count * in_width)
    offsets = jnp.abs(jnp.arange(2 * REACH + 1, dtype=jnp.int32) - REACH)
    keep = offsets[None, :] <= row_widths[:, None]
    masked = jnp.where(keep[:, None, None, :], disco_basis, jnp.zeros_like(disco_basis))
    span = cols_dev + 2 * REACH
    table = jnp.pad(masked, ((0, 0), (0, basis_count), (0, 0), (0, span - masked.shape[3])))
    table = table.reshape(rows_dev * 2 * basis_count, 3 * span).astype(jnp.float32)
    lanes = -(-3 * span // 128) * 128
    table = jnp.pad(table, ((0, 0), (0, lanes - 3 * span)))
    own_width = channels // lax.axis_size("ch")
    sizes = (lax.axis_size("lat"), lax.axis_size("lon"))
    plan = (rows_dev, cols_dev, basis_count, layers)
    outs = run_net(
        plan,
        sizes,
        latent_in,
        encoder_weight,
        table,
        block_weights,
        cotangent.reshape(cell_count, channels),
    )
    current, gradient = (field.reshape(rows_dev, cols_dev, channels) for field in outs[:2])
    sums = [value.astype(jnp.float32) for value in outs[2:]]
    block_sum, encoder_sum = jnp.stack(sums[:-1]), sums[-1]
    cells_total = cell_count * lax.axis_size("lon") * lax.axis_size(("lat", "ch"))
    normalizer = 1.0 / math.sqrt(cells_total)
    block_grads = (block_sum * normalizer).reshape(layers, basis_count * channels, own_width)
    encoder_grad = encoder_sum * normalizer
    return (current, gradient, block_grads, encoder_grad)


def solution(mesh):
    placed = (
        P(("ens", "lat", "ch"), "lon", None),
        P(("lat", "ch"), None, None),
        P(("ens", "lat", "ch")),
        P(),
        P(("lat", "ch"), None, None, None),
        P(("lat", "ch")),
        P(),
        P(("ens", "lat", "ch"), "lon", None),
    )
    return jax.shard_map(
        per_device,
        mesh=mesh,
        in_specs=placed,
        out_specs=(
            P(("ens", "lat", "ch"), "lon", None),
            P(("ens", "lat", "ch"), "lon", None),
            P("ens", None, "ch"),
            P("ens", "ch"),
        ),
        check_vma=False,
    )
```

time: 205 us -> 89 us (0.43)
  blocking collectives: 74.7 us -> 0 us
  Pallas kernels: 0 us -> 60.7 us
  waiting for transfers between devices: 39.8 us -> 2.88 us
  starting transfers between devices: 42.6 us -> 7.95 us
  between operations: 14.7 us -> 0.88 us
  matrix products: 8.68 us -> 0.25 us
  local copies, waits for them, and re-layouts: 15.9 us -> 10.1 us
    psum x1 -> x0, blocking collectives: 74.7 us -> none  [per_device(): lax.psum((block_part, encoder_part), ('lon', 'lat'))]
    pallas_call x0 -> x1, Pallas kernels: none -> 60.7 us  [run_net(): pl.pallas_call(functools.partial(net_kernel, plan), out_shape=[field, fie...]
    unnamed x4 -> x0, waiting for transfers between devices: 17.9 us -> none
    ppermute x5 -> x1, starting transfers between devices: 12.4 us -> 2.09 us  [padded(): lax.ppermute(lax.slice_in_dim(block, 0, width, axis=dim), axis, backward)]
    ppermute x6 -> x2, starting transfers between devices: 11.3 us -> 2.75 us  [from_behind(): return lax.ppermute(block, axis, route)]
    dot_general x21 -> x0, matrix products: 8.43 us -> none  [the longest x2 2.08 us: per_device(): jnp.dot(features, block_weights[layer_index], preferred_element_type=jnp....]
    ppermute x4 -> x0, starting transfers between devices: 7.87 us -> none  [passed_along(): return lax.ppermute(value, axis, pairs)]
    ppermute x5 -> x1, starting transfers between devices: 11 us -> 3.1 us  [padded(): lax.ppermute(lax.slice_in_dim(block, block.shape[dim] - width, None, axis...]
  transfers between devices with their start and end apart: 22 -> 4, of which waited for: 12 -> 1; matrix products, arithmetic and copies ran while one was open for 5% -> 4% of each run, Pallas kernels for 0% -> 0%
where the time goes in v2:
time: 89 us; the launch traced here: 88.6 us
  Pallas kernels  60.7 us (68%)
  local copies, waits for them, and re-layouts  10.1 us (11%)
  starting transfers between devices  7.95 us (9%)
  other arithmetic  5.87 us (7%)
  waiting for transfers between devices  2.88 us (3%)
    pallas_call x1, Pallas kernels, run_net(): pl.pallas_call(functools.partial(net_kernel, plan), out_shape=[field, fie...  60.7 us
    slice x5, local copies, waits for them, and re-layouts, per_device(): sampled = extended_in[:, tap_index:tap_index + cols_in:2, :]  3.65 us
    unnamed x19, local copies, waits for them, and re-layouts  3.61 us
    ppermute x1, starting transfers between devices, padded(): lax.ppermute(lax.slice_in_dim(block, block.shape[dim] - width, None, axis...  3.1 us
    ppermute x2, waiting for transfers between devices, from_behind(): return lax.ppermute(block, axis, route)  2.88 us
    ppermute x2, starting transfers between devices, from_behind(): return lax.ppermute(block, axis, route)  2.75 us
    ppermute x1, starting transfers between devices, padded(): lax.ppermute(lax.slice_in_dim(block, 0, width, axis=dim), axis, backward)  2.09 us
    mul x1, other arithmetic, per_device(): block_sum * normalizer  2.02 us
  transfers between devices with their start and end apart: 4, of which 1 were waited for; matrix products, arithmetic and copies ran while one was open for 4% of the time, Pallas kernels for 0%

profile of v2, /device:TPU:0, one launch (start us, length us, event | category | flops | bytes accessed | tf_op | source)
XLA Modules:
  0.0 88.6 jit_solution(4205261487097261368)
XLA Ops:
  0.6 0.0 copy-start.4
  0.6 0.9 %fusion.5 = (bf16[32,2,128]{2,1,0:T(2,128)(2,1)S(1)}, bf16[32,2,128]{2,1,0:T(2,128)(2,1)S(1)}) fusion(bf16[32,32,128]{2,1,0:T(8,128)(2,1)} %param.8), kind=kLoop, calls=%fused_computation.21 | loop fusion | bytes 65536 | tf_op jit(solution)/shard_map/slice | solution.py:469
  1.6 0.0 copy-start.5
  1.6 3.1 %collective-permute-start = (bf16[32,2,128]{2,1,0:T(2,128)(2,1)S(1)}, bf16[32,2,128]{2,1,0:T(2,128)(2,1)S(1)}, u32[]{:S(2)}, u32[]{:S(2)}) collective-permute-start(bf16[32,2,128]{2,1,0:T(2,128)(2,1)S(1)} %get-tuple-element.16), channel_id=1, source_target_pairs={{0,4},{4,8},{8,12},{12,0},{1,5},{5,9},{9,13},{13,1},{2,6},{6,10},{... | collective-permute-start | bytes 49160 | tf_op jit(solution)/shard_map/ppermute | solution.py:468
  4.7 2.1 %collective-permute-start.1 = (bf16[32,2,128]{2,1,0:T(2,128)(2,1)S(1)}, bf16[32,2,128]{2,1,0:T(2,128)(2,1)S(1)}, u32[]{:S(2)}, u32[]{:S(2)}) collective-permute-start(bf16[32,2,128]{2,1,0:T(2,128)(2,1)S(1)} %get-tuple-element.17), channel_id=1, source_target_pairs={{4,0},{8,4},{12,8},{0,12},{5,1},{9,5},{13,9},{1,13},{6,2},{10,6},{... | collective-permute-start | bytes 49160 | tf_op jit(solution)/shard_map/ppermute | solution.py:471
  6.8 0.0 copy-done.5
  6.8 0.0 copy-start.6
  6.8 0.6 copy-done.6
  7.5 0.1 broadcast_compare_fusion
  7.5 0.0 copy-done.4
  7.6 0.6 copy-done.7
  8.2 1.8 %slice.53 = bf16[32,16,128]{2,1,0:T(8,128)(2,1)S(1)} slice(bf16[32,32,128]{2,1,0:T(8,128)(2,1)} %param.8), slice={[0:32:1], [0:32:2], [0:128:1]} | slice | bytes 262144 | tf_op jit(solution)/shard_map/slice | solution.py:506
  10.0 0.1 copy.18
  10.1 0.1 copy.19
  10.2 0.1 copy.20
  10.3 0.1 copy.21
  10.4 0.1 copy.22
  10.5 0.0 copy-start
  10.5 0.1 pad.28.clone
  10.6 0.1 convert_element_type.60
  10.7 0.0 collective-permute-done
  10.7 0.0 collective-permute-done.1
  10.7 0.7 copy-done
  11.4 0.2 pad_maximum_fusion
  11.6 0.4 slice.49
  12.0 0.4 slice.51
  12.4 0.5 slice.55
  12.9 0.5 slice.57
  13.6 1.0 %add_convert_fusion = bf16[32,16,4,128]{3,2,1,0:T(4,128)(2,1)S(1)} fusion(f32[32,4]{1,0:T(8,128)S(1)} %copy.22, f32[32,16,128]{2,1,0:T(8,128)S(1)} %convert_element_type.57, f32[32,4]{1,0:T(8,128)S(1)} %copy.21, f32[32,16,128]{2,1,0:T(8,128)S(1)} %convert_element_type.56, f32[32,4]{1,0:T(8,128)S(1)} %copy.20, f32[32,16,128]{2,1,0:T(8,128)S(1)} %convert_element_type.55, ...), kind=kLoop, calls=%fused_computation | loop fusion | flops 2621440 | bytes 1837568 | tf_op jit(solution)/shard_map/convert_element_type | solution.py:512
  14.6 0.4 reshape.91
  15.0 0.2 fusion.6
  15.3 0.1 fusion.4
  15.3 1.5 %collective-permute-start.2 = (bf16[1,8192]{1,0:T(2,128)(2,1)S(1)}, bf16[1,8192]{1,0:T(2,128)(2,1)S(1)}, u32[]{:S(2)}, u32[]{:S(2)}) collective-permute-start(bf16[1,8192]{1,0:T(2,128)(2,1)S(1)} %get-tuple-element.14), channel_id=1, source_target_pairs={{0,1},{1,2},{2,3},{4,5},{5,6},{6,7},{8,9},{9,10},{10,11},{12,13},{... | collective-permute-start | bytes 49160 | tf_op jit(solution)/shard_map/ppermute | solution.py:458
  16.8 1.3 %collective-permute-start.3 = (bf16[1,8192]{1,0:T(2,128)(2,1)S(1)}, bf16[1,8192]{1,0:T(2,128)(2,1)S(1)}, u32[]{:S(2)}, u32[]{:S(2)}) collective-permute-start(bf16[1,8192]{1,0:T(2,128)(2,1)S(1)} %get-tuple-element.15), channel_id=1, source_target_pairs={{1,0},{2,1},{3,2},{5,4},{6,5},{7,6},{9,8},{10,9},{11,10},{13,12},{... | collective-permute-start | bytes 49160 | tf_op jit(solution)/shard_map/ppermute | solution.py:458
  18.1 0.6 pad_convert_fusion.refs_2_
  18.7 0.0 collective-permute-done.2
  18.7 2.9 %collective-permute-done.3 = bf16[1,8192]{1,0:T(2,128)(2,1)S(1)} collective-permute-done((bf16[1,8192]{1,0:T(2,128)(2,1)S(1)}, bf16[1,8192]{1,0:T(2,128)(2,1)S(1)}, u32[]{:S(2)}, u32[]{:S(2)}) %collective-permute-start.3) | collective-permute-done | bytes 16416 | tf_op jit(solution)/shard_map/ppermute | solution.py:458
  21.6 0.1 fusion.1
  21.7 0.8 reshape.86.refs_0_
  22.6 60.7 %shard_map.111 = (bf16[256,256]{1,0:T(8,128)(2,1)}, bf16[256,256]{1,0:T(8,128)(2,1)}, bf16[1024,128]{1,0:T(8,128)(2,1)}, bf16[1024,128]{1,0:T(8,128)(2,1)}, bf16[512,128]{1,0:T(8,128)(2,1)}) custom-call(bf16[256,512]{1,0:T(8,128)(2,1)} %reshape.86.refs_0_, bf16[512,256]{1,0:T(8,128)(2,1)} %refs_1_.1, f32[128,128]{1,0:T(8,128)} %pad_convert_fusion.refs_2_, ...), custom_call_target="tpu_custom_call" | custom-call | tf_op jit(solution)/shard_map/pallas_call | solution.py:443
  83.3 0.0 copy-start.1
  83.3 1.7 %convert_multiply_fusion.1 = f32[512,128]{1,0:T(8,128)} fusion(bf16[512,128]{1,0:T(8,128)(2,1)} %get-tuple-element.13), kind=kLoop, calls=%fused_computation.6 | loop fusion | flops 131072 | bytes 393216 | tf_op jit(solution)/shard_map/mul | solution.py:555
  85.0 0.0 copy-done.1
  85.0 2.0 %convert_multiply_fusion = f32[2,1024,128]{2,1,0:T(8,128)} fusion(bf16[1,1024,128]{2,1,0:T(8,128)(2,1)} %bitcast.17, bf16[1,1024,128]{2,1,0:T(8,128)(2,1)S(1)} %bitcast.16), kind=kLoop, calls=%fused_computation.1 | loop fusion | flops 786432 | bytes 1572864 | tf_op jit(solution)/shard_map/mul | solution.py:554
  87.0 0.0 copy-done.3
  87.0 0.7 copy.27
  87.7 0.3 copy-done.2
  88.0 0.7 copy.28
  (14 shorter events, 0.2 us)
Async XLA Ops:
  0.6 6.9 %copy-start.4 = (bf16[16,4,3,17]{3,1,2,0:T(4,128)(2,1)S(1)}, bf16[16,4,3,17]{3,1,2,0:T(4,128)(2,1)}, u32[]{:S(2)}) copy-start(bf16[16,4,3,17]{3,1,2,0:T(4,128)(2,1)} %param.12) | copy-start | bytes 19588
  1.6 5.2 %copy-start.5 = (bf16[32,4,5]{0,1,2:T(4,128)(2,1)S(1)}, bf16[32,4,5]{0,1,2:T(4,128)(2,1)}, u32[]{:S(2)}) copy-start(bf16[32,4,5]{0,1,2:T(4,128)(2,1)} %param.9) | copy-start | bytes 3844
  1.6 9.1 %collective-permute-start = (bf16[32,2,128]{2,1,0:T(2,128)(2,1)S(1)}, bf16[32,2,128]{2,1,0:T(2,128)(2,1)S(1)}, u32[]{:S(2)}, u32[]{:S(2)}) collective-permute-start(bf16[32,2,128]{2,1,0:T(2,128)(2,1)S(1)} %get-tuple-element.16), channel_id=1, source_target_pairs={{0,4},{4,8},{8,12},{12,0},{1,5},{5,9},{9,13},{13,1},{2,6},{6,10},{... | collective-permute-start | bytes 49160 | tf_op jit(solution)/shard_map/ppermute | solution.py:468
  4.7 6.1 %collective-permute-start.1 = (bf16[32,2,128]{2,1,0:T(2,128)(2,1)S(1)}, bf16[32,2,128]{2,1,0:T(2,128)(2,1)S(1)}, u32[]{:S(2)}, u32[]{:S(2)}) collective-permute-start(bf16[32,2,128]{2,1,0:T(2,128)(2,1)S(1)} %get-tuple-element.17), channel_id=1, source_target_pairs={{4,0},{8,4},{12,8},{0,12},{5,1},{9,5},{13,9},{1,13},{6,2},{10,6},{... | collective-permute-start | bytes 49160 | tf_op jit(solution)/shard_map/ppermute | solution.py:471
  6.8 0.7 copy-start.6
  7.5 0.7 copy-start.7
  10.5 1.0 %copy-start = (bf16[32,32,128]{2,1,0:T(8,128)(2,1)S(1)}, bf16[32,32,128]{2,1,0:T(8,128)(2,1)}, u32[]{:S(2)}) copy-start(bf16[32,32,128]{2,1,0:T(8,128)(2,1)} %param.8) | copy-start | bytes 786436
  15.3 3.4 %collective-permute-start.2 = (bf16[1,8192]{1,0:T(2,128)(2,1)S(1)}, bf16[1,8192]{1,0:T(2,128)(2,1)S(1)}, u32[]{:S(2)}, u32[]{:S(2)}) collective-permute-start(bf16[1,8192]{1,0:T(2,128)(2,1)S(1)} %get-tuple-element.14), channel_id=1, source_target_pairs={{0,1},{1,2},{2,3},{4,5},{5,6},{6,7},{8,9},{9,10},{10,11},{12,13},{... | collective-permute-start | bytes 49160 | tf_op jit(solution)/shard_map/ppermute | solution.py:458
  16.8 4.8 %collective-permute-start.3 = (bf16[1,8192]{1,0:T(2,128)(2,1)S(1)}, bf16[1,8192]{1,0:T(2,128)(2,1)S(1)}, u32[]{:S(2)}, u32[]{:S(2)}) collective-permute-start(bf16[1,8192]{1,0:T(2,128)(2,1)S(1)} %get-tuple-element.15), channel_id=1, source_target_pairs={{1,0},{2,1},{3,2},{5,4},{6,5},{7,6},{9,8},{10,9},{11,10},{13,12},{... | collective-permute-start | bytes 49160 | tf_op jit(solution)/shard_map/ppermute | solution.py:458
  83.3 1.7 %copy-start.1 = (bf16[1024,128]{1,0:T(8,128)(2,1)S(1)}, bf16[1024,128]{1,0:T(8,128)(2,1)}, u32[]{:S(2)}) copy-start(bf16[1024,128]{1,0:T(8,128)(2,1)} %get-tuple-element.11) | copy-start | bytes 786436
  85.0 2.0 %copy-start.3 = (bf16[256,256]{1,0:T(8,128)(2,1)S(1)}, bf16[256,256]{1,0:T(8,128)(2,1)}, u32[]{:S(2)}) copy-start(bf16[256,256]{1,0:T(8,128)(2,1)} %get-tuple-element.9) | copy-start | bytes 393220
  87.0 1.0 %copy-start.2 = (bf16[256,256]{1,0:T(8,128)(2,1)S(1)}, bf16[256,256]{1,0:T(8,128)(2,1)}, u32[]{:S(2)}) copy-start(bf16[256,256]{1,0:T(8,128)(2,1)} %get-tuple-element.10) | copy-start | bytes 393220

commit v3 on v2

--- a/solution.py
+++ b/solution.py
@@ -74,27 +74,32 @@
     def __init__(self, result, bufs):
         super().__init__(bufs[-2:])
         self.result = result
-        self.source, self.rec_ch, self.part, self.rec_lat, self.strip, self.rec_lon, self.piece = bufs[:-2]
+        self.source, self.rec_ch, self.part, self.rec_lat, self.strip, self.rec_pair, self.half, self.rec_far, self.piece = bufs[:-2]
         self.width = self.part.shape[1]
         self.lat, self.lon = lax.axis_size("lat"), lax.axis_size("lon")
         self.height = self.strip.shape[0]
         self.span = self.piece.shape[0]
-        self.split = self.span < self.height
+        self.pair = self.height // self.span
+        self.far = self.lon // self.pair
+        self.side = lax.rem(lax.axis_index("lon"), self.pair)
 
     @staticmethod
     def scratch(sizes, rows, columns):
         lat, lon = sizes
         width = columns // 2
         height = rows // lat
-        span = height // lon if height % (lon * TILE) == 0 else height
-        count = 1 + 2 * (lat - 1) + 2 * (lon - 1)
+        pair = 2 if lon % 2 == 0 and height % (2 * TILE) == 0 else 1
+        span, far = height // pair, lon // pair
+        count = 1 + 2 * (lat - 1) + 2 * (pair - 1) + far - 1
         return [
             pltpu.VMEM((rows, columns), BF16),
             pltpu.VMEM((rows, width), BF16),
             pltpu.VMEM((rows, width), BF16),
             pltpu.VMEM((lat - 1, height, width), BF16),
             pltpu.VMEM((height, width), BF16),
-            pltpu.VMEM((lon - 1, span, width), BF16),
+            pltpu.VMEM((span, width), BF16),
+            pltpu.VMEM((span, width), BF16),
+            pltpu.VMEM((far - 1, span, width), BF16),
             pltpu.VMEM((span, width), BF16),
             pltpu.SemaphoreType.DMA((count,)),
             pltpu.SemaphoreType.DMA((count,)),
@@ -126,44 +131,46 @@
         for step in range(1, self.lat):
             total = total + self.rec_lat[step - 1].astype(F32)
         self.strip[...] = total.astype(BF16)
-        for step in range(1, self.lon):
-            peer = along("lon", step)
-            source = self.strip
-            if self.split:
-                source = self.strip.at[self.stretch(peer["lon"], self.span)]
-            self.send(source, self.rec_lon.at[step - 1], self.lat + step - 1, peer)
+        if self.pair > 1:
+            rows = self.stretch(1 - self.side, self.span)
+            self.send(self.strip.at[rows], self.rec_pair, self.lat, along("lon", 1 - 2 * self.side))
+
+    def start_far(self):
+        self.settle()
+        total = self.strip[self.stretch(self.side, self.span), :].astype(F32)
+        if self.pair > 1:
+            total = total + self.rec_pair[...].astype(F32)
+        self.half[...] = total.astype(BF16)
+        for step in range(1, self.far):
+            self.send(
+                self.half, self.rec_far.at[step - 1], self.lat + step, along("lon", self.pair * step)
+            )
 
     def gather_lon(self):
         self.settle()
-        if self.split:
-            total = self.strip[self.stretch(lax.axis_index("lon"), self.span), :].astype(F32)
-        else:
-            total = self.strip[...].astype(F32)
-        for step in range(1, self.lon):
-            total = total + self.rec_lon[step - 1].astype(F32)
+        total = self.half[...].astype(F32)
+        for step in range(1, self.far):
+            total = total + self.rec_far[step - 1].astype(F32)
         self.piece[...] = total.astype(BF16)
-        offset = lax.axis_index("lat") * self.height
-        if self.split:
-            offset = offset + lax.axis_index("lon") * self.span
+        offset = lax.axis_index("lat") * self.height + self.side * self.span
         rows = pl.ds(pl.multiple_of(offset, TILE), self.span)
         self.result[rows, :] = self.piece[...]
-        if self.split:
-            for step in range(1, self.lon):
-                slot = self.lat + self.lon - 2 + step
-                self.send(self.piece, self.result.at[rows], slot, along("lon", step))
+        if self.pair > 1:
+            slot = self.lat + self.far
+            self.send(self.piece, self.result.at[rows], slot, along("lon", 1 - 2 * self.side))
 
     def gather_lat(self):
         self.settle()
         rows = self.stretch(lax.axis_index("lat"), self.height)
         for step in range(1, self.lat):
-            slot = self.lat + 2 * self.lon - 3 + step
+            slot = self.lat + self.far + self.pair - 2 + step
             self.send(self.result.at[rows], self.result.at[rows], slot, along("lat", step))
 
     def finish(self):
         self.settle()
 
 
-STAGES = ("start_ch", "start_lat", "start_lon", "gather_lon", "gather_lat", "finish")
+STAGES = ("start_ch", "start_lat", "start_lon", "start_far", "gather_lon", "gather_lat", "finish")
 
 
 class Halo(Sender):
@@ -346,24 +353,167 @@
 
 def rows_product(left, right):
     return lax.dot_general(left, right, (((0,), (0,)), ((), ())), preferred_element_type=F32)
+TAPS_LEFT = TAP_REACH
+
+
+class InputHalo(Sender):
+    def __init__(self, bufs):
+        super().__init__(bufs[-2:])
+        (
+            self.edges,
+            self.out_cols,
+            self.out_table,
+            self.in_cols,
+            self.in_row,
+            self.in_table,
+            self.in_tile,
+        ) = bufs[:-2]
+
+    @staticmethod
+    def scratch(rows_in, cols_in, width, table_rows, lanes):
+        return [
+            pltpu.VMEM((3, rows_in, width), F32),
+            pltpu.VMEM((3, rows_in, width), BF16),
+            pltpu.VMEM((2, table_rows, lanes), F32),
+            pltpu.VMEM((3, rows_in, width), BF16),
+            pltpu.VMEM((2, cols_in, width), BF16),
+            pltpu.VMEM((2, table_rows, lanes), F32),
+            pltpu.VMEM((4, TILE, width), BF16),
+            pltpu.SemaphoreType.DMA((10,)),
+            pltpu.SemaphoreType.DMA((10,)),
+        ]
+
+    def start(self, field, table, owner, rows_in, cols_in):
+        first = own_first_row(rows_in // 2)
+        table_rows = self.out_table.shape[1]
+        for block, row, target in ((0, 0, first - 1), (1, rows_in - 1, first + rows_in // 2)):
+            feeds = jnp.where(owner[row] == target, 1.0, 0.0)
+            self.out_table[block] = table[row * table_rows : (row + 1) * table_rows, :] * feeds
+        last = (rows_in - 1) * cols_in
+        lines = (field.at[pl.ds(0, cols_in)], field.at[pl.ds(last, cols_in)])
+        slot = 0
+        for block, row_step in ((0, -1), (1, 1)):
+            self.send(lines[block], self.in_row.at[1 - block], slot, neighbour(row_step, 0))
+            base = block * last
+            west = field.at[pl.ds(base, TILE)]
+            east = field.at[pl.ds(base + cols_in - TILE, TILE)]
+            place = 2 * (1 - block)
+            self.send(west, self.in_tile.at[place + 1], slot + 1, neighbour(row_step, -1))
+            self.send(east, self.in_tile.at[place], slot + 2, neighbour(row_step, 1))
+            slot += 3
+
+        def one(row):
+            low = field[pl.ds(pl.multiple_of(row * cols_in, TILE), TILE), :].astype(F32)
+            start = pl.multiple_of(row * cols_in + cols_in - TILE, TILE)
+            high = field[pl.ds(start, TILE), :].astype(F32)
+            self.edges[0, pl.ds(row, 1), :] = high[TILE - 2 : TILE - 1]
+            self.edges[1, pl.ds(row, 1), :] = high[TILE - 1 : TILE]
+            self.edges[2, pl.ds(row, 1), :] = low[0:1]
+
+        over_rows(rows_in, one)
+        self.out_cols[...] = self.edges[...].astype(BF16)
+        self.send(self.out_cols.at[pl.ds(0, 2)], self.in_cols.at[pl.ds(0, 2)], 6, neighbour(0, 1))
+        self.send(self.out_cols.at[2], self.in_cols.at[2], 7, neighbour(0, -1))
+        self.send(self.out_table.at[0], self.in_table.at[1], 8, neighbour(-1, 0))
+        self.send(self.out_table.at[1], self.in_table.at[0], 9, neighbour(1, 0))
+
+
+def own_first_row(rows):
+    return (lax.axis_index("lat") * lax.axis_size("ch") + lax.axis_index("ch")) * rows
+
+
+def tap_matrix(table, basis_count, cols, cols_in):
+    lanes = table.shape[1]
+    blocks = []
+    for k in range(basis_count):
+        line = jnp.broadcast_to(table[k : k + 1], (cols, lanes))
+        moved = pltpu.roll(line, 0, 1, stride=2, stride_axis=0)
+        wrapped = pltpu.roll(moved, cols_in + TILE - TAPS_LEFT, 1)
+        moved = pltpu.roll(moved, lanes - TAPS_LEFT, 1)
+        lane = lax.broadcasted_iota(jnp.int32, (cols, lanes), 1)
+        at_end = (lane >= cols_in + TILE - TAPS_LEFT) & (lane < cols_in + TILE)
+        blocks.append(jnp.where(at_end, wrapped, moved))
+    return jnp.concatenate(blocks, axis=0)[:, : cols_in + TILE].astype(BF16)
+
+
+def filtered_row(table, line, left_two, left_one, right, basis_count, cols, cols_in):
+    width = line.shape[1]
+    place = lax.broadcasted_iota(jnp.int32, (TILE, width), 0)
+    tile = jnp.where(place == 0, jnp.broadcast_to(right, (TILE, width)), 0.0)
+    tile = jnp.where(place == TILE - 2, jnp.broadcast_to(left_two, (TILE, width)), tile)
+    tile = jnp.where(place == TILE - 1, jnp.broadcast_to(left_one, (TILE, width)), tile)
+    rhs = jnp.concatenate([line, tile.astype(BF16)], axis=0)
+    lhs = tap_matrix(table, basis_count, cols, cols_in)
+    return jnp.dot(lhs, rhs, preferred_element_type=F32).astype(BF16)
+
+
+def finish_encode(halo, field, table, owner, filtered, latent_in, plan, rows_in, cols_in):
+    rows, cols, basis_count, _ = plan
+    table_rows = halo.out_table.shape[1]
+    block = basis_count * cols
+    width = field.shape[1]
+    halo.settle()
+    halo.edges[...] = halo.in_cols[...].astype(F32)
+
+    def one(row):
+        sides = [halo.edges[index, pl.ds(row, 1), :] for index in range(3)]
+        line = field[aligned(row, cols_in), :]
+        taps = table[aligned(row, table_rows), :]
+        filtered[aligned(row + 1, block), :] = filtered_row(
+            taps, line, *sides, basis_count, cols, cols_in
+        )
+
+    over_rows(rows_in, one)
+    for side, row in ((0, 0), (1, rows_in + 1)):
+        west = halo.in_tile[2 * side].astype(F32)
+        east = halo.in_tile[2 * side + 1].astype(F32)
+        filtered[row * block : (row + 1) * block, :] = filtered_row(
+            halo.in_table[side],
+            halo.in_row[side],
+            west[TILE - 2 : TILE - 1],
+            west[TILE - 1 : TILE],
+            east[0:1],
+            basis_count,
+            cols,
+            cols_in,
+        )
+    first = own_first_row(rows)
+    for row in range(rows):
+        total = None
+        for offset in range(-1, 3):
+            source = 2 * row + offset
+            term = filtered[(source + 1) * block : (source + 2) * block, :].astype(F32)
+            if 0 <= source < rows_in:
+                term = term * jnp.where(owner[source] == first + row, 1.0, 0.0)
+            total = term if total is None else total + term
+        total = total.astype(BF16)
+        for k in range(basis_count):
+            latent_in[row * cols : (row + 1) * cols, k * width : (k + 1) * width] = total[
+                k * cols : (k + 1) * cols
+            ]
+
+
+def lanes_of(count):
+    return -(-(count + 2 * TILE) // 128) * 128
 
 
 def net_kernel(plan, *refs):
     rows, cols, basis_count, layers = plan
-    latent_in, encoder_weight, base, weights, cotangent = refs[:5]
-    state_out, latent_grad = refs[5:7]
-    results = refs[7 : 8 + layers]
-    rest = list(refs[8 + layers :])
-    bands, ext, spread, errs, features, preact = rest[:6]
-    rest = rest[6:]
+    field, table, owner, encoder_weight, base, weights, cotangent = refs[:7]
+    state_out, latent_grad = refs[7:9]
+    results = refs[9 : 10 + layers]
+    rest = list(refs[10 + layers :])
+    bands, ext, spread, errs, features, preact, filtered, latent_in = rest[:8]
+    input_halo = InputHalo(rest[8:17])
+    rest = rest[17:]
     halos = []
     for _ in range(2 * layers):
         halos.append(Halo(rest[:6]))
         rest = rest[6:]
     sums = []
     for index in range(layers + 1):
-        sums.append(GradSum(results[index], rest[:9]))
-        rest = rest[9:]
+        sums.append(GradSum(results[index], rest[:11]))
+        rest = rest[11:]
     channels = ext.shape[1]
     progress = [0] * (layers + 1)
 
@@ -372,12 +522,15 @@
         progress[index] += 1
 
     greet()
+    rows_in = owner.shape[0]
+    cols_in = field.shape[0] // rows_in
+    input_halo.start(field, table, owner, rows_in, cols_in)
+    make_bands(base, bands, rows, cols, basis_count)
+    finish_encode(input_halo, field, table, owner, filtered, latent_in, plan, rows_in, cols_in)
     state = jnp.dot(latent_in[...], encoder_weight[...], preferred_element_type=F32)
     state = state.astype(BF16).astype(F32)
     for layer in range(layers):
         send_state(halos[layer], state, rows, cols)
-        if layer == 0:
-            make_bands(base, bands, rows, cols, basis_count)
         halos[layer].settle()
         extend(halos[layer], state, ext, rows, cols)
         stencil(bands, ext, features.at[layer], rows, cols, basis_count)
@@ -418,11 +571,12 @@
                 advance(index)
 
 
-def run_net(plan, sizes, latent_in, encoder_weight, base, weights, cotangent):
+def run_net(plan, sizes, field_in, table, owner, encoder_weight, base, weights, cotangent):
     rows, cols, basis_count, layers = plan
     cells, channels = rows * cols, weights.shape[2]
     features = basis_count * channels
     span = cols + 2 * REACH
+    rows_in = owner.shape[0]
     in_features = encoder_weight.shape[0]
     heights = [features] * layers + [in_features]
     scratch = [
@@ -432,7 +586,12 @@
         pltpu.VMEM((rows * basis_count * cols, channels), BF16),
         pltpu.VMEM((layers, cells, features), BF16),
         pltpu.VMEM((layers, cells, channels), F32),
+        pltpu.VMEM(((rows_in + 2) * basis_count * cols, field_in.shape[1]), BF16),
+        pltpu.VMEM((cells, in_features), BF16),
     ]
+    scratch += InputHalo.scratch(
+        rows_in, field_in.shape[0] // rows_in, field_in.shape[1], table.shape[0] // rows_in, table.shape[1]
+    )
     for index in range(2 * layers):
         scratch += Halo.scratch(rows, cols, channels, 2 if index < layers else 4)
     for height in heights:
@@ -443,42 +602,13 @@
     return pl.pallas_call(
         functools.partial(net_kernel, plan),
         out_shape=[field, field] + grads,
-        in_specs=[vmem] * 5,
+        in_specs=[vmem, vmem, pl.BlockSpec(memory_space=pltpu.SMEM)] + [vmem] * 4,
         out_specs=[vmem] * (3 + layers),
         scratch_shapes=scratch,
         compiler_params=pltpu.CompilerParams(
             collective_id=0, has_side_effects=True, vmem_limit_bytes=56 << 20
         ),
-    )(latent_in, encoder_weight, base, weights, cotangent)
-
-
-def from_behind(block, axis, distance):
-    devices = range(lax.axis_size(axis))
-    route = [(i - distance, i) for i in devices if i - distance in devices]
-    return lax.ppermute(block, axis, route)
-
-
-def padded(block, sides, width, periodic):
-    for axis, dim in sides:
-        count = lax.axis_size(axis)
-        forward = [(i, i + 1) for i in range(count - 1)]
-        if periodic:
-            forward.append((count - 1, 0))
-        backward = [(target, source) for source, target in forward]
-        low = lax.ppermute(
-            lax.slice_in_dim(block, block.shape[dim] - width, None, axis=dim), axis, forward
-        )
-        high = lax.ppermute(lax.slice_in_dim(block, 0, width, axis=dim), axis, backward)
-        block = jnp.concatenate([low, block, high], axis=dim)
-    return block
-
-
-def add_edges(middle, to_first, to_last):
-    row_count = middle.shape[0]
-    rest_pads = [(0, 0)] * (middle.ndim - 1)
-    lower = jnp.pad(to_first, [(0, row_count - 1)] + rest_pads)
-    upper = jnp.pad(to_last, [(row_count - 1, 0)] + rest_pads)
-    return middle + lower + upper
+    )(field_in, table, owner, encoder_weight, base, weights, cotangent)
 
 
 def per_device(
@@ -499,48 +629,27 @@
     channels = block_weights.shape[2]
     layers = block_weights.shape[0]
     cell_count = rows_dev * cols_dev
-    extended_in = padded(input_field, (("lon", 1),), TAP_REACH, True)
-    filter_values = encoder_filter.astype(jnp.float32)
-    accumulated = jnp.zeros((rows_in, cols_dev, basis_count, in_width), jnp.float32)
-    for tap_index in range(tap_count):
-        sampled = extended_in[:, tap_index : tap_index + cols_in : 2, :]
-        accumulated = (
-            accumulated
-            + sampled[:, :, None, :].astype(jnp.float32)
-            * filter_values[:, None, :, tap_index, None]
-        )
-    filtered_in = accumulated.astype(jnp.bfloat16).reshape(
-        rows_in, cols_dev * basis_count * in_width
-    )
-    first_row = lax.axis_index(("lat", "ch")) * rows_dev
-    relative = row_owner - first_row + 1
-    selector = (relative[None, :] == jnp.arange(rows_dev + 2, dtype=jnp.int32)[:, None]).astype(
-        jnp.bfloat16
-    )
-    summed = jnp.dot(selector, filtered_in, preferred_element_type=jnp.float32)
-    from_above = from_behind(summed[0:1].astype(jnp.bfloat16), ("lat", "ch"), -1).astype(
-        jnp.float32
-    )
-    from_below = from_behind(summed[rows_dev + 1 :].astype(jnp.bfloat16), ("lat", "ch"), 1).astype(
-        jnp.float32
-    )
-    regridded = add_edges(summed[1 : rows_dev + 1], from_below, from_above)
-    latent_in = regridded.astype(jnp.bfloat16).reshape(cell_count, basis_count * in_width)
     offsets = jnp.abs(jnp.arange(2 * REACH + 1, dtype=jnp.int32) - REACH)
     keep = offsets[None, :] <= row_widths[:, None]
     masked = jnp.where(keep[:, None, None, :], disco_basis, jnp.zeros_like(disco_basis))
     span = cols_dev + 2 * REACH
     table = jnp.pad(masked, ((0, 0), (0, basis_count), (0, 0), (0, span - masked.shape[3])))
     table = table.reshape(rows_dev * 2 * basis_count, 3 * span).astype(jnp.float32)
-    lanes = -(-3 * span // 128) * 128
+    lanes = lanes_of(2 * span)
     table = jnp.pad(table, ((0, 0), (0, lanes - 3 * span)))
+    taps = jnp.pad(
+        encoder_filter.astype(jnp.float32),
+        ((0, 0), (0, basis_count), (0, lanes_of(cols_in) - tap_count)),
+    ).reshape(rows_in * 2 * basis_count, -1)
     own_width = channels // lax.axis_size("ch")
     sizes = (lax.axis_size("lat"), lax.axis_size("lon"))
     plan = (rows_dev, cols_dev, basis_count, layers)
     outs = run_net(
         plan,
         sizes,
-        latent_in,
+        input_field.reshape(rows_in * cols_in, in_width),
+        taps,
+        row_owner,
         encoder_weight,
         table,
         block_weights,

time: 89 us -> 77 us (0.87)
  starting transfers between devices: 7.95 us -> 0 us
  Pallas kernels: 60.7 us -> 68.1 us
  local copies, waits for them, and re-layouts: 10.1 us -> 2.87 us
  waiting for transfers between devices: 2.88 us -> 0 us
    ppermute x4 -> x0, starting transfers between devices: 7.95 us -> none  [the longest x1 3.1 us: padded(): lax.ppermute(lax.slice_in_dim(block, block.shape[dim] - width, None, axis...]
    pallas_call x1, Pallas kernels: 60.7 us -> 68.1 us  [run_net(): pl.pallas_call(functools.partial(net_kernel, plan), out_shape=[field, fie...]
    slice x7 -> x0, local copies, waits for them, and re-layouts: 4.62 us -> none  [the longest x5 3.65 us: per_device(): sampled = extended_in[:, tap_index:tap_index + cols_in:2, :]]
    ppermute x4 -> x0, waiting for transfers between devices: 2.88 us -> none  [the longest x2 2.88 us: from_behind(): return lax.ppermute(block, axis, route)]
    convert_element_type x8 -> x0, other arithmetic: 1.26 us -> none  [the longest x1 1.03 us: per_device(): accumulated.astype(jnp.bfloat16)]
    mul x1, other arithmetic: 1.67 us -> 0.72 us  [per_device(): encoder_grad = encoder_sum * normalizer]
    unnamed x19 -> x14, local copies, waits for them, and re-layouts: 3.61 us -> 2.7 us
  transfers between devices with their start and end apart: 4 -> 0, of which waited for: 1 -> 0; matrix products, arithmetic and copies ran while one was open for 4% -> 0% of each run, Pallas kernels for 0% -> 0%
where the time goes in v3:
time: 77 us; the launch traced here: 76.7 us
  Pallas kernels  68.1 us (88%)
  other arithmetic  5.05 us (7%)
  local copies, waits for them, and re-layouts  2.87 us (4%)
    pallas_call x1, Pallas kernels, run_net(): pl.pallas_call(functools.partial(net_kernel, plan), out_shape=[field, fie...  68.1 us
    unnamed x14, local copies, waits for them, and re-layouts  2.7 us
    mul x1, other arithmetic, per_device(): block_sum * normalizer  2.1 us

profile of v3, /device:TPU:0, one launch (start us, length us, event | category | flops | bytes accessed | tf_op | source)
XLA Modules:
  0.0 76.7 jit_solution(14773741459708767396)
XLA Ops:
  0.6 0.0 copy-start.4
  0.7 0.6 copy-done.4
  1.3 0.1 broadcast_compare_fusion
  1.4 0.8 %broadcast_select_fusion = bf16[16,4,3,17]{3,1,2,0:T(4,128)(2,1)S(1)} fusion(bf16[16,4,3,17]{3,1,2,0:T(4,128)(2,1)} %param.12, pred[16,17]{1,0:T(8,128)(4,1)S(1)} %broadcast_compare_fusion), kind=kLoop, calls=%fused_computation.3 | loop fusion | flops 3264 | bytes 13328 | tf_op jit(solution)/shard_map/jit(_where)/select_n | solution.py:634
  2.2 0.1 pad.16.clone
  2.3 0.1 convert_element_type.16
  2.4 0.0 copy-start.3
  2.4 0.6 pad_convert_fusion.refs_4_
  3.1 0.0 copy-done.3
  3.1 0.1 copy.16
  3.2 0.7 bitcast_convert_fusion.refs_1_
  3.9 68.1 %shard_map.111 = (bf16[256,256]{1,0:T(8,128)(2,1)}, bf16[256,256]{1,0:T(8,128)(2,1)}, bf16[1024,128]{1,0:T(8,128)(2,1)}, bf16[1024,128]{1,0:T(8,128)(2,1)}, bf16[512,128]{1,0:T(8,128)(2,1)}) custom-call(bf16[1024,128]{1,0:T(8,128)(2,1)} %bitcast.9, f32[256,128]{1,0:T(8,128)} %bitcast_convert_fusion.refs_1_, s32[32]{0:T(128)} %refs_2_.1, ...), custom_call_target="tpu_custom_call" | custom-call | tf_op jit(solution)/shard_map/pallas_call | solution.py:602
  72.0 0.0 copy-start
  72.0 2.1 %convert_multiply_fusion = f32[2,1024,128]{2,1,0:T(8,128)} fusion(bf16[1,1024,128]{2,1,0:T(8,128)(2,1)} %bitcast.11, bf16[1,1024,128]{2,1,0:T(8,128)(2,1)} %bitcast.10), kind=kLoop, calls=%fused_computation | loop fusion | flops 786432 | bytes 1572864 | tf_op jit(solution)/shard_map/mul | solution.py:663
  74.1 0.0 copy-done
  74.1 0.0 copy-start.2
  74.1 0.7 convert_multiply_fusion.1
  74.8 0.3 copy-done.2
  75.1 0.0 copy-start.1
  75.1 0.7 copy.21
  75.7 0.3 copy-done.1
  76.0 0.7 copy.22
  (2 shorter events, 0.0 us)
Async XLA Ops:
  0.6 0.7 copy-start.4
  2.4 0.7 copy-start.3
  72.0 2.1 %copy-start = (bf16[512,128]{1,0:T(8,128)(2,1)S(1)}, bf16[512,128]{1,0:T(8,128)(2,1)}, u32[]{:S(2)}) copy-start(bf16[512,128]{1,0:T(8,128)(2,1)} %get-tuple-element.13) | copy-start | bytes 393220
  74.1 1.0 %copy-start.2 = (bf16[256,256]{1,0:T(8,128)(2,1)S(1)}, bf16[256,256]{1,0:T(8,128)(2,1)}, u32[]{:S(2)}) copy-start(bf16[256,256]{1,0:T(8,128)(2,1)} %get-tuple-element.9) | copy-start | bytes 393220
  75.1 1.0 %copy-start.1 = (bf16[256,256]{1,0:T(8,128)(2,1)S(1)}, bf16[256,256]{1,0:T(8,128)(2,1)}, u32[]{:S(2)}) copy-start(bf16[256,256]{1,0:T(8,128)(2,1)} %get-tuple-element.10) | copy-start | bytes 393220

commit v4 on v3

--- a/solution.py
+++ b/solution.py
@@ -293,7 +293,7 @@
     return pl.ds(pl.multiple_of(index * size, size), size)
 
 
-GROUP = 4
+GROUP = 16
 
 
 def over_rows(rows, body):
@@ -556,17 +556,18 @@
         halo = halos[layers + layer]
         send_spread(halo, spread, rows, cols)
         sums[layer].source[...] = rows_product(features[layer], act_grad).astype(BF16)
-        advance(layer)
-        if layer + 1 < layers:
-            advance(layer + 1)
+        for other in range(layers - 1, layer - 1, -1):
+            advance(other)
         halo.settle()
+        for other in range(layers - 1, layer - 1, -1):
+            advance(other)
         lines = take_spread(halo, spread, gradient, rows, cols)
         gradient = jnp.concatenate(lines, axis=0).astype(BF16).astype(F32)
     latent_grad[...] = gradient.astype(BF16)
     sums[layers].source[...] = rows_product(latent_in[...], gradient.astype(BF16)).astype(BF16)
     advance(layers)
     while min(progress) < len(STAGES):
-        for index in list(range(layers))[::-1] + [layers]:
+        for index in [layers] + list(range(layers))[::-1]:
             if progress[index] < len(STAGES):
                 advance(index)
 

time: 77 us -> 73.4 us (0.953)
  Pallas kernels: 68.1 us -> 64.5 us
    pallas_call x1, Pallas kernels: 68.1 us -> 64.5 us  [run_net(): pl.pallas_call(functools.partial(net_kernel, plan), out_shape=[field, fie...]
where the time goes in v4:
time: 73.4 us; the launch traced here: 73.1 us
  Pallas kernels  64.5 us (88%)
  other arithmetic  5.05 us (7%)
  local copies, waits for them, and re-layouts  2.87 us (4%)
    pallas_call x1, Pallas kernels, run_net(): pl.pallas_call(functools.partial(net_kernel, plan), out_shape=[field, fie...  64.5 us
    unnamed x14, local copies, waits for them, and re-layouts  2.7 us
    mul x1, other arithmetic, per_device(): block_sum * normalizer  2.1 us

profile of v4, /device:TPU:0, one launch (start us, length us, event | category | flops | bytes accessed | tf_op | source)
XLA Modules:
  0.0 73.1 jit_solution(8087386098013807156)
XLA Ops:
  0.6 0.0 copy-start.4
  0.7 0.6 copy-done.4
  1.3 0.1 broadcast_compare_fusion
  1.4 0.8 %broadcast_select_fusion = bf16[16,4,3,17]{3,1,2,0:T(4,128)(2,1)S(1)} fusion(bf16[16,4,3,17]{3,1,2,0:T(4,128)(2,1)} %param.12, pred[16,17]{1,0:T(8,128)(4,1)S(1)} %broadcast_compare_fusion), kind=kLoop, calls=%fused_computation.3 | loop fusion | flops 3264 | bytes 13328 | tf_op jit(solution)/shard_map/jit(_where)/select_n | solution.py:635
  2.2 0.1 pad.16.clone
  2.3 0.1 convert_element_type.16
  2.4 0.0 copy-start.3
  2.4 0.6 pad_convert_fusion.refs_4_
  3.1 0.0 copy-done.3
  3.1 0.1 copy.16
  3.2 0.7 bitcast_convert_fusion.refs_1_
  3.9 64.5 %shard_map.111 = (bf16[256,256]{1,0:T(8,128)(2,1)}, bf16[256,256]{1,0:T(8,128)(2,1)}, bf16[1024,128]{1,0:T(8,128)(2,1)}, bf16[1024,128]{1,0:T(8,128)(2,1)}, bf16[512,128]{1,0:T(8,128)(2,1)}) custom-call(bf16[1024,128]{1,0:T(8,128)(2,1)} %bitcast.9, f32[256,128]{1,0:T(8,128)} %bitcast_convert_fusion.refs_1_, s32[32]{0:T(128)} %refs_2_.1, ...), custom_call_target="tpu_custom_call" | custom-call | tf_op jit(solution)/shard_map/pallas_call | solution.py:603
  68.4 0.0 copy-start
  68.4 2.1 %convert_multiply_fusion = f32[2,1024,128]{2,1,0:T(8,128)} fusion(bf16[1,1024,128]{2,1,0:T(8,128)(2,1)} %bitcast.11, bf16[1,1024,128]{2,1,0:T(8,128)(2,1)} %bitcast.10), kind=kLoop, calls=%fused_computation | loop fusion | flops 786432 | bytes 1572864 | tf_op jit(solution)/shard_map/mul | solution.py:664
  70.5 0.0 copy-done
  70.5 0.0 copy-start.2
  70.5 0.7 convert_multiply_fusion.1
  71.3 0.3 copy-done.2
  71.5 0.0 copy-start.1
  71.5 0.7 copy.21
  72.2 0.3 copy-done.1
  72.5 0.7 copy.22
  (2 shorter events, 0.0 us)
Async XLA Ops:
  0.6 0.7 copy-start.4
  2.4 0.7 copy-start.3
  68.4 2.1 %copy-start = (bf16[512,128]{1,0:T(8,128)(2,1)S(1)}, bf16[512,128]{1,0:T(8,128)(2,1)}, u32[]{:S(2)}) copy-start(bf16[512,128]{1,0:T(8,128)(2,1)} %get-tuple-element.13) | copy-start | bytes 393220
  70.5 1.0 %copy-start.2 = (bf16[256,256]{1,0:T(8,128)(2,1)S(1)}, bf16[256,256]{1,0:T(8,128)(2,1)}, u32[]{:S(2)}) copy-start(bf16[256,256]{1,0:T(8,128)(2,1)} %get-tuple-element.9) | copy-start | bytes 393220
  71.5 1.0 %copy-start.1 = (bf16[256,256]{1,0:T(8,128)(2,1)S(1)}, bf16[256,256]{1,0:T(8,128)(2,1)}, u32[]{:S(2)}) copy-start(bf16[256,256]{1,0:T(8,128)(2,1)} %get-tuple-element.10) | copy-start | bytes 393220
